TPU v7x, 512 devices: a whole 4x8x8 slice. The times are simulated.
512 devices in a mesh: dp: 16 (over z, core), tp: 4 (over y_lo), cp: 8 (over y_hi, x).
Axes of the slice: x: 4, y: 8 (y_hi: 2, y_lo: 4; y = y_hi * 4 + y_lo), z: 8, core: 2. Of those that a mesh axis runs over, the one named last changes fastest.
Arguments:
- tokens: bfloat16 [65536, 1024], P(('dp', 'tp', 'cp')), may hold values from -6 to 6
- expert_ids: int32 [65536, 2], P(('dp', 'tp', 'cp')), may hold values from 0 to 31, all different within a row; in each aligned block of 128 rows (0 to 127, 128 to 255, ...) at most 12 rows name the same one
- router_weight: bfloat16 [1024, 32], replicated, may hold values from -0.1875 to 0.1875
- gate_weight: bfloat16 [32, 1024, 384], P(('tp', 'cp'), 'dp'), may hold values from -0.1875 to 0.1875
- up_weight: bfloat16 [32, 1024, 384], P(('tp', 'cp'), 'dp'), may hold values from -0.1875 to 0.1875
- down_weight: bfloat16 [32, 384, 1024], P(('tp', 'cp'), None, 'dp'), may hold values from -0.3125 to 0.3125
- grad_out: bfloat16 [65536, 1024], P(('dp', 'tp', 'cp')), may hold values from -6 to 6
Outputs:
- moe_out: bfloat16 [65536, 1024], P(('dp', 'tp', 'cp'))
- grad_tokens: bfloat16 [65536, 1024], P(('dp', 'tp', 'cp'))
- router_grad: float32 [1024, 32], replicated
Inputs may be any that keep to these rules, and one draw needn't show every extreme that they name: `expert_ids`: each row names 2 different experts. Among the 128 rows of one device no expert is named by more than 12 rows, a bound that some block reaches.
All inputs are finite; a program needn't handle non-finite values.
Results may differ from a plain program's by a relative error of at most 0.0064.
Values may be sent and summed in bfloat16 or wider, within the bound.
A program may use at most 64 MiB of HBM per device.

v0:
```python
import jax
import jax.numpy as jnp
from jax import lax
from jax.sharding import PartitionSpec as P


def route_slots(flat_ids, expert_count):
    hits = (flat_ids[:, None] == jnp.arange(expert_count, dtype=jnp.int32)[None, :]).astype(
        jnp.int32
    )
    before = jnp.cumsum(hits, axis=0) - hits
    return jnp.sum(before * hits, axis=1)


def trade(stacked, capacity):
    item_count = stacked.shape[0]
    feature_dim = stacked.shape[2]
    tp_count = lax.axis_size("tp")
    cp_count = lax.axis_size("cp")
    shaped = stacked.reshape(item_count, tp_count * cp_count, capacity, feature_dim)
    moved = lax.all_to_all(shaped, ("tp", "cp"), split_axis=1, concat_axis=1, tiled=True)
    return moved.reshape(item_count, -1, feature_dim)


def expert_forward(received, w_gate, w_up, w_down):
    gate_act = jnp.dot(received, w_gate, preferred_element_type=jnp.float32)
    up_act = jnp.dot(received, w_up, preferred_element_type=jnp.float32)
    hidden = (jax.nn.silu(gate_act) * up_act).astype(jnp.bfloat16)
    produced = jnp.dot(hidden, w_down, preferred_element_type=jnp.float32).astype(jnp.bfloat16)
    return (gate_act, up_act, produced)


def expert_backward(received_grad, gate_act, up_act, w_gate, w_up, w_down):
    contract = (((1,), (1,)), ((), ()))
    grad_hidden = lax.dot_general(
        received_grad, w_down, contract, preferred_element_type=jnp.float32
    )
    sigma = jax.nn.sigmoid(gate_act)
    grad_gate = (grad_hidden * up_act * sigma * (1.0 + gate_act * (1.0 - sigma))).astype(
        jnp.bfloat16
    )
    grad_up = (grad_hidden * gate_act * sigma).astype(jnp.bfloat16)
    returned = lax.dot_general(grad_gate, w_gate, contract, preferred_element_type=jnp.float32)
    returned = returned + lax.dot_general(
        grad_up, w_up, contract, preferred_element_type=jnp.float32
    )
    return returned.astype(jnp.bfloat16)


def on_device(tokens, expert_ids, router_weight, gate_weight, up_weight, down_weight, grad_out):
    row_count, feature_dim = tokens.shape
    topk = expert_ids.shape[1]
    groups = lax.axis_size(("tp", "cp"))
    capacity = 3 * row_count * topk // (2 * groups)
    expert_count = router_weight.shape[1]
    contract = (((1,), (1,)), ((), ()))
    w_gate, w_up, w_down = (
        lax.all_gather(gate_weight[0], "dp", axis=0, tiled=True),
        lax.all_gather(up_weight[0], "dp", axis=0, tiled=True),
        lax.all_gather(down_weight[0], "dp", axis=1, tiled=True),
    )
    logits = jnp.dot(tokens, router_weight, preferred_element_type=jnp.float32)
    chosen = jnp.take_along_axis(logits, expert_ids, axis=1)
    mixing = 1.0 / jnp.sum(jnp.exp(chosen[:, None, :] - chosen[:, :, None]), axis=2)
    flat_ids = expert_ids.reshape(-1)
    slots = route_slots(flat_ids, expert_count)
    position = flat_ids * capacity + slots
    slot_total = groups * capacity
    repeated = jnp.repeat(tokens, topk, axis=0)
    scaled_grad = (mixing[:, :, None] * grad_out.astype(jnp.float32)[:, None, :]).astype(
        jnp.bfloat16
    )
    scaled_flat = scaled_grad.reshape(-1, feature_dim)
    sent = jnp.zeros((1, slot_total, feature_dim), jnp.bfloat16).at[0, position].set(repeated)
    received = trade(sent, capacity)[0]
    gate_act, up_act, produced = expert_forward(received, w_gate, w_up, w_down)
    came_back = trade(produced[None], capacity)[0]
    sent_grad = (
        jnp.zeros((1, slot_total, feature_dim), jnp.bfloat16).at[0, position].set(scaled_flat)
    )
    received_grad = trade(sent_grad, capacity)[0]
    returned = expert_backward(received_grad, gate_act, up_act, w_gate, w_up, w_down)
    back_home = trade(returned[None], capacity)[0]
    out_rows = jnp.take(came_back, position, axis=0).reshape(row_count, topk, feature_dim)
    moe_out = jnp.sum(mixing[:, :, None] * out_rows.astype(jnp.float32), axis=1).astype(
        jnp.bfloat16
    )
    back_rows = jnp.take(back_home, position, axis=0).reshape(row_count, topk, feature_dim)
    scores = jnp.einsum("td,tkd->tk", grad_out, out_rows, preferred_element_type=jnp.float32)
    dlogit = mixing * (scores - jnp.sum(mixing * scores, axis=1, keepdims=True))
    onehot = (
        expert_ids[:, :, None] == jnp.arange(expert_count, dtype=jnp.int32)[None, None, :]
    ).astype(jnp.float32)
    dense = jnp.sum(onehot * dlogit[:, :, None], axis=1).astype(jnp.bfloat16)
    router_back = lax.dot_general(
        dense, router_weight, contract, preferred_element_type=jnp.float32
    )
    grad_tokens = (jnp.sum(back_rows.astype(jnp.float32), axis=1) + router_back).astype(
        jnp.bfloat16
    )
    router_part = lax.dot_general(
        tokens, dense, (((0,), (0,)), ((), ())), preferred_element_type=jnp.float32
    )
    router_grad = lax.psum(router_part, ("dp", "tp", "cp"))
    return (moe_out, grad_tokens, router_grad)


def solution(mesh):
    in_specs = (
        P(("dp", "tp", "cp"), None),
        P(("dp", "tp", "cp"), None),
        P(),
        P(("tp", "cp"), "dp", None),
        P(("tp", "cp"), "dp", None),
        P(("tp", "cp"), None, "dp"),
        P(("dp", "tp", "cp"), None),
    )
    out_specs = (P(("dp", "tp", "cp"), None), P(("dp", "tp", "cp"), None), P())
    return jax.shard_map(
        on_device, mesh=mesh, in_specs=in_specs, out_specs=out_specs, check_vma=False
    )
```

profile of v0, /device:TPU:1, one launch (start us, length us, event | category | flops | bytes accessed | tf_op | source)
XLA Modules:
  0.0 453.8 jit_solution(12045069232960749352)
XLA Ops:
  7.2 0.7 broadcast_multiply_fusion
  7.9 0.8 copy.57
  10.1 1.2 broadcast_in_dim.16
  11.6 1.9 scatter_custom_fusion
  13.5 1.2 reshape.105
  14.7 10.6 %all-to-all-start = ((bf16[1,32,12,1024]{3,2,0,1:T(8,128)(2,1)}), bf16[1,32,12,1024]{3,2,0,1:T(8,128)(2,1)S(1)}, u32[]{:S(2)}, u32[]{:S(2)}) async-start(bf16[1,32,12,1024]{3,2,0,1:T(8,128)(2,1)} %bitcast.4), calls=%async_computation | async-start | bytes 2097152 | tf_op jit(solution)/shard_map/all_to_all | solution.py:21
  25.3 27.5 %all-gather.2 = bf16[1,384,1024]{1,2,0:T(8,128)(2,1)} all-gather(bf16[1,384,64]{1,2,0:T(8,128)(2,1)S(1)} %copy-done.15), channel_id=4, replica_groups=mesh['dp'=16,'tp'=4,'cp'=8] {'dp'}, dimensions={2}, use_global_device_ids=true | all-gather | bytes 835584 | tf_op jit(solution)/shard_map/all_gather | solution.py:60
  52.9 16.6 %all-gather.1 = bf16[1,1024,384]{2,1,0:T(8,128)(2,1)S(1)} all-gather(bf16[1,64,384]{2,1,0:T(8,128)(2,1)S(1)} %copy-done.16), channel_id=3, replica_groups=mesh['dp'=16,'tp'=4,'cp'=8] {'dp'}, dimensions={1}, use_global_device_ids=true | all-gather | bytes 835584 | tf_op jit(solution)/shard_map/all_gather | solution.py:59
  69.5 17.9 %all-gather = bf16[1,1024,384]{2,1,0:T(8,128)(2,1)S(1)} all-gather(bf16[1,64,384]{2,1,0:T(8,128)(2,1)S(1)} %copy-done.17), channel_id=2, replica_groups=mesh['dp'=16,'tp'=4,'cp'=8] {'dp'}, dimensions={1}, use_global_device_ids=true | all-gather | bytes 835584 | tf_op jit(solution)/shard_map/all_gather | solution.py:58
  89.1 0.8 copy-done.10
  90.5 1.2 reshape_broadcast_in_dim.6
  91.8 9.6 %all-to-all-start.1 = ((bf16[1,32,12,1024]{3,2,0,1:T(8,128)(2,1)}), bf16[1,32,12,1024]{3,2,0,1:T(8,128)(2,1)S(1)}, u32[]{:S(2)}, u32[]{:S(2)}) async-start(bf16[1,32,12,1024]{3,2,0,1:T(8,128)(2,1)} %bitcast.8), calls=%async_computation.1 | async-start | bytes 2097152 | tf_op jit(solution)/shard_map/all_to_all | solution.py:21
  101.9 2.0 gather_fusion
  104.4 1.7 mul.98
  106.1 21.9 %all-to-all-done.1 = bf16[1,32,12,1024]{3,2,0,1:T(8,128)(2,1)S(1)} async-done(((bf16[1,32,12,1024]{3,2,0,1:T(8,128)(2,1)}), bf16[1,32,12,1024]{3,2,0,1:T(8,128)(2,1)S(1)}, u32[]{:S(2)}, u32[]{:S(2)}) %all-to-all-start.1) | async-done | bytes 786464 | tf_op jit(solution)/shard_map/all_to_all | solution.py:21
  128.3 1.2 gather_fusion.1
  129.8 1.1 fusion.13
  131.3 2.0 scatter_custom_fusion.1
  133.5 33.6 %all_to_all.20 = bf16[1,32,12,1024]{3,2,0,1:T(8,128)(2,1)S(1)} all-to-all(bf16[1,32,12,1024]{3,2,0,1:T(8,128)(2,1)S(1)} %bitcast.72), channel_id=1, replica_groups=mesh['dp'=16,'tp'=4,'cp'=8] {'tp','cp'}, dimensions={1} | all-to-all | bytes 1572864 | tf_op jit(solution)/shard_map/all_to_all | solution.py:21
  167.3 1.8 fusion.1
  169.1 0.7 fusion.7
  170.9 1.2 reshape_broadcast_in_dim.7
  172.1 6.0 %all-to-all-start.3 = ((bf16[1,32,12,1024]{3,2,0,1:T(8,128)(2,1)}), bf16[1,32,12,1024]{3,2,0,1:T(8,128)(2,1)S(1)}, u32[]{:S(2)}, u32[]{:S(2)}) async-start(bf16[1,32,12,1024]{3,2,0,1:T(8,128)(2,1)} %bitcast.10), calls=%async_computation.3 | async-start | bytes 2097152 | tf_op jit(solution)/shard_map/all_to_all | solution.py:21
  178.2 0.8 convolution_bitcast_fusion
  179.0 2.1 multiply_reduce_fusion
  181.2 22.9 %all-to-all-done.3 = bf16[1,32,12,1024]{3,2,0,1:T(8,128)(2,1)S(1)} async-done(((bf16[1,32,12,1024]{3,2,0,1:T(8,128)(2,1)}), bf16[1,32,12,1024]{3,2,0,1:T(8,128)(2,1)S(1)}, u32[]{:S(2)}, u32[]{:S(2)}) %all-to-all-start.3) | async-done | bytes 786464 | tf_op jit(solution)/shard_map/all_to_all | solution.py:21
  204.2 1.2 gather_fusion.2
  205.5 0.6 reshape.108
  206.1 1.2 reduce_sum.60
  207.4 1.0 fusion
  208.3 237.0 %all-reduce.3.cloned.1.call-done = f32[1024,32]{0,1:T(8,128)} async-done(((f32[1024,32]{0,1:T(8,128)}), f32[1024,32]{0,1:T(8,128)}) %all-reduce.3.cloned.1.call-update) | async-done | bytes 131088 | tf_op jit(solution)/shard_map/psum | solution.py:104
  445.3 1.6 copy.73
  (81 shorter events, 7.6 us)
Async XLA Ops:
  7.2 94.5 %copy-start = (bf16[1024,32]{0,1:T(8,128)(2,1)S(1)}, bf16[1024,32]{0,1:T(8,128)(2,1)}, u32[]{:S(2)}) copy-start(bf16[1024,32]{0,1:T(8,128)(2,1)} %param.11) | copy-start | bytes 196612
  13.5 11.8 %copy-start.15 = (bf16[1,384,64]{1,2,0:T(8,128)(2,1)S(1)}, bf16[1,384,64]{1,2,0:T(8,128)(2,1)}, u32[]{:S(2)}) copy-start(bf16[1,384,64]{1,2,0:T(8,128)(2,1)} %param.14) | copy-start | bytes 147460
  14.7 38.2 %copy-start.16 = (bf16[1,64,384]{2,1,0:T(8,128)(2,1)S(1)}, bf16[1,64,384]{2,1,0:T(8,128)(2,1)}, u32[]{:S(2)}) copy-start(bf16[1,64,384]{2,1,0:T(8,128)(2,1)} %param.13) | copy-start | bytes 147460
  14.7 54.8 %copy-start.17 = (bf16[1,64,384]{2,1,0:T(8,128)(2,1)S(1)}, bf16[1,64,384]{2,1,0:T(8,128)(2,1)}, u32[]{:S(2)}) copy-start(bf16[1,64,384]{2,1,0:T(8,128)(2,1)} %param.12) | copy-start | bytes 147460
  14.7 72.7 %all-to-all-start = ((bf16[1,32,12,1024]{3,2,0,1:T(8,128)(2,1)}), bf16[1,32,12,1024]{3,2,0,1:T(8,128)(2,1)S(1)}, u32[]{:S(2)}, u32[]{:S(2)}) async-start(bf16[1,32,12,1024]{3,2,0,1:T(8,128)(2,1)} %bitcast.4), calls=%async_computation | async-start | bytes 2097152 | tf_op jit(solution)/shard_map/all_to_all | solution.py:21
  69.5 18.7 %copy-start.2 = (bf16[1,1024,384]{2,1,0:T(8,128)(2,1)}, bf16[1,1024,384]{2,1,0:T(8,128)(2,1)S(1)}, u32[]{:S(2)}) copy-start(bf16[1,1024,384]{2,1,0:T(8,128)(2,1)S(1)} %all-gather.1) | copy-start | bytes 2359300
  87.4 0.9 copy-start.4
  88.3 0.8 copy-start.12
  88.3 1.6 copy-start.6
  89.1 0.8 copy-start.10
  90.5 10.9 %copy-start.18 = (s32[128,2]{0,1:T(2,128)S(1)}, s32[128,2]{0,1:T(2,128)}, u32[]{:S(2)}) copy-start(s32[128,2]{0,1:T(2,128)} %param.10) | copy-start | bytes 3076
  91.8 9.9 %copy-start.7 = (bf16[128,1024]{1,0:T(8,128)(2,1)S(1)}, bf16[128,1024]{1,0:T(8,128)(2,1)}, u32[]{:S(2)}) copy-start(bf16[128,1024]{1,0:T(8,128)(2,1)} %param.9) | copy-start | bytes 786436
  91.8 36.3 %all-to-all-start.1 = ((bf16[1,32,12,1024]{3,2,0,1:T(8,128)(2,1)}), bf16[1,32,12,1024]{3,2,0,1:T(8,128)(2,1)S(1)}, u32[]{:S(2)}, u32[]{:S(2)}) async-start(bf16[1,32,12,1024]{3,2,0,1:T(8,128)(2,1)} %bitcast.8), calls=%async_computation.1 | async-start | bytes 2097152 | tf_op jit(solution)/shard_map/all_to_all | solution.py:21
  101.9 2.2 copy-start.14
  129.8 1.2 copy-start.8
  129.8 1.5 copy-start.1
  167.1 2.0 copy-start.5
  167.3 1.8 copy-start.11
  167.3 1.8 copy-start.13
  169.1 1.1 copy-start.3
  172.1 6.9 %copy-start.9 = (bf16[128,2,1024]{2,1,0:T(2,128)(2,1)S(1)}, bf16[128,2,1024]{2,1,0:T(2,128)(2,1)}, u32[]{:S(2)}) copy-start(bf16[128,2,1024]{2,1,0:T(2,128)(2,1)} %copy-done.8) | copy-start | bytes 1572868
  172.1 32.0 %all-to-all-start.3 = ((bf16[1,32,12,1024]{3,2,0,1:T(8,128)(2,1)}), bf16[1,32,12,1024]{3,2,0,1:T(8,128)(2,1)S(1)}, u32[]{:S(2)}, u32[]{:S(2)}) async-start(bf16[1,32,12,1024]{3,2,0,1:T(8,128)(2,1)} %bitcast.10), calls=%async_computation.3 | async-start | bytes 2097152 | tf_op jit(solution)/shard_map/all_to_all | solution.py:21
  178.1 267.3 %all-reduce.3.cloned.1.call-start = ((), (), s32[]{:S(2)}) async-start(), calls=%async_computation.4 | async-start | bytes 262144 | tf_op jit(solution)/shard_map/psum | solution.py:104
Sparse Core Ops, SparseCore 0:
  184.5 260.8 all-reduce.2
where the time goes:
time: 454 us
  waiting for transfers between devices  282 us (62%)
  blocking collectives  95.7 us (21%)
  starting transfers between devices  26.3 us (6%)
  local copies, waits for them, and re-layouts  20.4 us (4%)
  between operations  14.4 us (3%)
  matrix products  7.95 us (2%)
  other arithmetic  7.16 us (2%)
    psum x1, waiting for transfers between devices, on_device(): router_grad = lax.psum(router_part, ('dp', 'tp', 'cp'))  237 us
    all_to_all x3, waiting for transfers between devices, trade(): lax.all_to_all(shaped, ('tp', 'cp'), split_axis=1, concat_axis=1, tiled=T...  44.8 us
    all_to_all x1, blocking collectives, trade(): lax.all_to_all(shaped, ('tp', 'cp'), split_axis=1, concat_axis=1, tiled=T...  33.6 us
    all_gather x1, blocking collectives, on_device(): lax.all_gather(down_weight[0], 'dp', axis=1, tiled=True)  27.5 us
    all_to_all x3, starting transfers between devices, trade(): lax.all_to_all(shaped, ('tp', 'cp'), split_axis=1, concat_axis=1, tiled=T...  26.3 us
    all_gather x1, blocking collectives, on_device(): lax.all_gather(gate_weight[0], 'dp', axis=0, tiled=True)  17.9 us
    all_gather x1, blocking collectives, on_device(): lax.all_gather(up_weight[0], 'dp', axis=0, tiled=True)  16.6 us
  transfers between devices with their start and end apart: 4, of which 3 were waited for; matrix products, arithmetic and copies ran while one was open for 3% of the time, Pallas kernels for 0%

commit v1 on v0

v1 whole, which is shorter than its diff:
```python
import functools

import jax
import jax.numpy as jnp
from jax import lax
from jax.experimental import pallas as pl
from jax.experimental.pallas import tpu as pltpu
from jax.sharding import PartitionSpec as P

MESH = pl.DeviceIdType.MESH
F32 = jnp.float32
BF16 = jnp.bfloat16
ROWS = 16
CAP = 12
LANES = 128


def iota(shape, dim):
    return lax.broadcasted_iota(jnp.int32, shape, dim)


def mm(a, b):
    return lax.dot_general(a, b, (((1,), (0,)), ((), ())), preferred_element_type=F32)


def mm_t(a, b):
    return lax.dot_general(a, b, (((1,), (1,)), ((), ())), preferred_element_type=F32)


def kernel(
    sizes,
    tok_ref, ids_ref, rw_ref, wg_ref, wu_ref, wd_ref, g_ref,
    moe_ref, gt_ref, rg_ref,
    sx, sg, rx, rg, px, pg, cx, cg, act, up, w, part, r1, ax, ay, fin,
    s_in, r_in, s_out, r_out, s_ring, r_ring, s_pair, r_pair, s_ar, r_ar,
):
    dpn, tpn, cpn = sizes
    groups = tpn * cpn
    half = groups // 2
    nx = cpn // 2
    nz = dpn // 2
    t_count, d = tok_ref.shape
    q = d // 4
    dp = lax.axis_index("dp")
    tp = lax.axis_index("tp")
    cp = lax.axis_index("cp")
    me = tp * cpn + cp
    xi = lax.rem(cp, nx)
    yh = cp // nx
    z = dp // 2
    core = lax.rem(dp, 2)

    def peer(r):
        to_tp = lax.rem(tp + lax.rem(r // nx, tpn), tpn)
        to_cp = lax.rem(yh + r // half, 2) * nx + lax.rem(xi + lax.rem(r, nx), nx)
        return to_tp, to_cp

    def mirror(r):
        back_x = lax.rem(nx - lax.rem(r, nx), nx)
        back_tp = lax.rem(tpn - lax.rem(r // nx, tpn), tpn)
        return (r // half) * half + back_tp * nx + back_x

    def remote(src, dst, send, recv, device):
        return pltpu.make_async_remote_copy(
            src_ref=src, dst_ref=dst, send_sem=send, recv_sem=recv,
            device_id=device, device_id_type=MESH,
        )

    def wait_bytes(ref, sem):
        pltpu.make_async_copy(ref, ref, sem).wait()

    barrier = pltpu.get_barrier_semaphore()

    def greet_plane(r, carry):
        to_tp, to_cp = peer(r)
        pl.semaphore_signal(barrier, inc=1, device_id=(dp, to_tp, to_cp), device_id_type=MESH)
        return carry

    def greet_dp(o, carry):
        pl.semaphore_signal(
            barrier, inc=1, device_id=(lax.rem(dp + o, dpn), tp, cp), device_id_type=MESH
        )
        return carry

    lax.fori_loop(1, groups, greet_plane, 0)
    lax.fori_loop(1, dpn, greet_dp, 0)

    tokens = tok_ref[...]
    grads = g_ref[...]
    lane = iota((t_count, LANES), 1)
    hot = [(lane == ids_ref[:, k : k + 1]).astype(F32) for k in range(2)]
    both = hot[0] + hot[1]
    both_t = both.T.astype(BF16)
    upper = (iota((t_count, t_count), 0) < iota((t_count, t_count), 1)).astype(BF16)
    before_t = mm(both_t, upper).astype(BF16)
    span = groups * ROWS
    spread_t = (iota((span, LANES), 0) // ROWS == iota((span, LANES), 1)).astype(BF16)
    slot_t = mm(spread_t, before_t)
    named_t = mm(spread_t, both_t) > 0.5
    row_t = lax.rem(iota((span, t_count), 0), ROWS)

    def choice(named, slot, row, j):
        wanted = row if j is None else jnp.where(row >= CAP, 3 * (row - CAP) + j, -1)
        return (named & (slot == wanted.astype(F32))).astype(BF16)

    main_t = choice(named_t, slot_t, row_t, None)
    tail_t = [choice(named_t, slot_t, row_t, j) for j in range(3)]

    def pack_home(values, out):
        for j in range(3):
            piece = mm(main_t, values[:, q * j : q * (j + 1)]) + mm(tail_t[j], values[:, 3 * q :])
            out[:, :, q * j : q * (j + 1)] = piece.astype(BF16).reshape(groups, ROWS, q)

    pack_home(tokens, sx)
    pack_home(grads, sg)

    shard = wg_ref.shape[1]
    eye = (iota((shard, shard), 0) == iota((shard, shard), 1)).astype(BF16)
    w[dp, 0] = wg_ref[0]
    w[dp, 1] = wu_ref[0]
    w[dp, 2] = mm_t(eye, wd_ref[0]).astype(BF16)

    pl.semaphore_wait(barrier, groups - 1 + dpn - 1)

    def ring(step, sign):
        slot = lax.rem(z - sign * step + nz, nz) * 2 + core
        index = step if sign > 0 else nz // 2 + step
        return remote(
            w.at[slot], w.at[slot], s_ring.at[index], r_ring.at[index],
            (lax.rem(z + sign + nz, nz) * 2 + core, tp, cp),
        )

    def pair(index, shift):
        slot = lax.rem(z + shift + nz, nz) * 2 + core
        return remote(
            w.at[slot], w.at[slot], s_pair.at[index], r_pair.at[index],
            (z * 2 + 1 - core, tp, cp),
        )

    rights, lefts = nz // 2, nz // 2 - 1
    right = [ring(s, 1) for s in range(rights)]
    left = [ring(s, -1) for s in range(lefts)]
    pairs = [pair(0, 0)]
    right[0].start()
    if lefts:
        left[0].start()
    pairs[0].start()

    def send_in(src, dst, phase):
        for h in range(2):
            def one(r, carry):
                to_tp, to_cp = peer(r)
                remote(
                    src.at[to_tp * cpn + to_cp], dst.at[mirror(r)],
                    s_in.at[2 * phase + h], r_in.at[2 * phase + h], (dp, to_tp, to_cp),
                ).start()
                return carry

            lax.fori_loop(max(1, half * h), half * (h + 1), one, 0)

    send_in(sx, rx, 0)
    send_in(sg, rg, 1)
    rx[0] = sx[me]
    rg[0] = sg[me]

    logits = mm(tokens, rw_ref[...])
    ecount = rw_ref.shape[1]
    chosen = [jnp.sum(logits * hot[k][:, :ecount], axis=1, keepdims=True) for k in range(2)]
    mixing = [
        1.0 / (1.0 + jnp.exp(chosen[1] - chosen[0])),
        1.0 / (1.0 + jnp.exp(chosen[0] - chosen[1])),
    ]
    lower = (iota((t_count, t_count), 1) < iota((t_count, t_count), 0)).astype(BF16)
    before = mm(lower, both.astype(BF16)).astype(BF16)
    spread = (iota((LANES, span), 1) // ROWS == iota((LANES, span), 0)).astype(BF16)
    slot = mm(before, spread)
    row = lax.rem(iota((t_count, span), 1), ROWS)
    picks = []
    for k in range(2):
        named = mm(hot[k].astype(BF16), spread) > 0.5
        picks.append([choice(named, slot, row, None)] + [choice(named, slot, row, j) for j in range(3)])

    for s in range(rights):
        right[s].wait_recv()
        if s + 1 < rights:
            right[s + 1].start()
        copy = pair(len(pairs), -(s + 1))
        copy.start()
        pairs.append(copy)
        if s < lefts:
            left[s].wait_recv()
            if s + 1 < lefts:
                left[s + 1].start()
            copy = pair(len(pairs), s + 1)
            copy.start()
            pairs.append(copy)
    for copy in pairs:
        copy.wait_recv()

    size = half * ROWS
    pr, qr = iota((size, size), 0), iota((size, size), 1)
    same = pr // ROWS == qr // ROWS
    pr, qr = lax.rem(pr, ROWS), lax.rem(qr, ROWS)
    unpack = [
        (same & (pr < CAP) & (qr >= CAP) & (pr == 3 * (qr - CAP) + j)).astype(BF16) for j in range(3)
    ]
    repack = [
        (same & (qr < CAP) & (pr >= CAP) & (qr == 3 * (pr - CAP) + j)).astype(BF16) for j in range(3)
    ]
    is_main = lax.rem(iota((size, q), 0), ROWS) < CAP

    def open_rows(ref, h):
        packed = ref[half * h : half * (h + 1)].reshape(size, 3 * q)
        tail = sum(mm(unpack[j], packed[:, q * j : q * (j + 1)]) for j in range(3))
        return jnp.concatenate([packed, tail.astype(BF16)], axis=1)

    def close_rows(values, ref, h):
        for j in range(3):
            piece = jnp.where(
                is_main, values[:, q * j : q * (j + 1)].astype(F32), mm(repack[j], values[:, 3 * q :])
            )
            ref[half * h : half * (h + 1), :, q * j : q * (j + 1)] = piece.astype(BF16).reshape(
                half, ROWS, q
            )

    def weight(i):
        return w[:, i].reshape(d, w.shape[3])

    def wait_in(ref, phase, h):
        lo = max(1, half * h)
        wait_bytes(ref.at[pl.ds(lo, half * (h + 1) - lo)], r_in.at[2 * phase + h])

    def send_out(src, dst, phase, h):
        def one(r, carry):
            to_tp, to_cp = peer(r)
            remote(
                src.at[r], dst.at[me], s_out.at[2 * phase + h], r_out.at[phase],
                (dp, to_tp, to_cp),
            ).start()
            return carry

        lax.fori_loop(max(1, half * h), half * (h + 1), one, 0)

    for h in range(2):
        wait_in(rx, 0, h)
        rows = open_rows(rx, h)
        gate = mm(rows, weight(0))
        upper_act = mm(rows, weight(1))
        act[size * h : size * (h + 1)] = gate
        up[size * h : size * (h + 1)] = upper_act
        hidden = (gate * jax.nn.sigmoid(gate) * upper_act).astype(BF16)
        close_rows(mm_t(hidden, weight(2)).astype(BF16), px, h)
        send_out(px, cx, 0, h)
    cx[me] = px[0]
    for h in range(2):
        wait_in(rg, 1, h)
        rows = open_rows(rg, h)
        grad_hidden = mm(rows, weight(2))
        gate = act[size * h : size * (h + 1)]
        upper_act = up[size * h : size * (h + 1)]
        sigma = jax.nn.sigmoid(gate)
        grad_gate = (grad_hidden * upper_act * sigma * (1.0 + gate * (1.0 - sigma))).astype(BF16)
        grad_up = (grad_hidden * gate * sigma).astype(BF16)
        back = mm_t(grad_gate, weight(0)) + mm_t(grad_up, weight(1))
        close_rows(back.astype(BF16), pg, h)
        send_out(pg, cg, 1, h)
    cg[me] = pg[0]

    def home_rows(ref, k):
        packed = ref[...].reshape(span, 3 * q)
        main = mm(picks[k][0], packed)
        tail = sum(mm(picks[k][1 + j], packed[:, q * j : q * (j + 1)]) for j in range(3))
        return jnp.concatenate([main, tail], axis=1)

    wait_bytes(cx.at[pl.ds(0, groups - 1)], r_out.at[0])
    grads32 = grads.astype(F32)
    total = None
    scores = []
    for k in range(2):
        rows = home_rows(cx, k)
        scores.append(jnp.sum(grads32 * rows, axis=1, keepdims=True))
        total = mixing[k] * rows if total is None else total + mixing[k] * rows
    moe_ref[...] = total.astype(BF16)
    mean = mixing[0] * scores[0] + mixing[1] * scores[1]
    dense = sum(hot[k] * (mixing[k] * (scores[k] - mean)) for k in range(2))
    dense_t = dense.T.astype(BF16)
    part[...] = mm(dense_t, tokens)[: part.shape[0]]

    cw = r1.shape[2]
    nb = d // cw

    def chunk(c):
        return pl.ds(pl.multiple_of(8 * (c // nb), 8), 8), pl.ds(
            pl.multiple_of(cw * lax.rem(c, nb), LANES), cw
        )

    def scatter(o, carry):
        to = lax.rem(dp + o, dpn)
        remote(part.at[chunk(to)], r1.at[o - 1], s_ar.at[0], r_ar.at[0], (to, tp, cp)).start()
        return carry

    lax.fori_loop(1, dpn, scatter, 0)

    router_back = mm_t(dense.astype(BF16)[:, :ecount], rw_ref[...])

    wait_bytes(r1, r_ar.at[0])
    rows_own, cols_own = chunk(dp)
    ax[xi] = jnp.sum(r1[...], axis=0) + part[rows_own, cols_own]
    for o in range(1, nx):
        remote(
            ax.at[xi], ax.at[xi], s_ar.at[1], r_ar.at[1],
            (dp, tp, yh * nx + lax.rem(xi + o, nx)),
        ).start()
    wait_bytes(ax.at[pl.ds(0, nx - 1)], r_ar.at[1])
    yn = 2 * tpn
    yi = yh * tpn + tp
    ay[yi] = jnp.sum(ax[...], axis=0)
    for o in range(1, yn):
        to = lax.rem(yi + o, yn)
        remote(
            ay.at[yi], ay.at[yi], s_ar.at[2], r_ar.at[2],
            (dp, lax.rem(to, tpn), (to // tpn) * nx + xi),
        ).start()
    wait_bytes(ay.at[pl.ds(0, yn - 1)], r_ar.at[2])
    fin[dp] = jnp.sum(ay[...], axis=0)

    def gather(o, carry):
        to = lax.rem(dp + o, dpn)
        remote(fin.at[dp], fin.at[dp], s_ar.at[3], r_ar.at[3], (to, tp, cp)).start()
        return carry

    lax.fori_loop(1, dpn, gather, 0)

    wait_bytes(cg.at[pl.ds(0, groups - 1)], r_out.at[1])
    gt_ref[...] = (
        mixing[0] * home_rows(cg, 0) + mixing[1] * home_rows(cg, 1) + router_back
    ).astype(BF16)

    wait_bytes(fin.at[pl.ds(0, dpn - 1)], r_ar.at[3])
    for c in range(dpn):
        rg_ref[8 * (c // nb) : 8 * (c // nb) + 8, cw * (c % nb) : cw * (c % nb + 1)] = fin[c]

    for phase, ref in enumerate((sx, sg)):
        for h in range(2):
            lo = max(1, half * h)
            wait_bytes(ref.at[pl.ds(lo, half * (h + 1) - lo)], s_in.at[2 * phase + h])
    for phase, ref in enumerate((px, pg)):
        for h in range(2):
            lo = max(1, half * h)
            wait_bytes(ref.at[pl.ds(lo, half * (h + 1) - lo)], s_out.at[2 * phase + h])
    for copy in right + left + pairs:
        copy.wait_send()
    wait_bytes(r1, s_ar.at[0])
    wait_bytes(ax.at[pl.ds(0, nx - 1)], s_ar.at[1])
    wait_bytes(ay.at[pl.ds(0, yn - 1)], s_ar.at[2])
    wait_bytes(fin.at[pl.ds(0, dpn - 1)], s_ar.at[3])


def on_device(tokens, expert_ids, router_weight, gate_weight, up_weight, down_weight, grad_out):
    sizes = tuple(lax.axis_size(name) for name in ("dp", "tp", "cp"))
    dpn, tpn, cpn = sizes
    groups = tpn * cpn
    t_count, d = tokens.shape
    shard, ff = gate_weight.shape[1:]
    block = pltpu.VMEM((groups, ROWS, 3 * d // 4), BF16)
    wide = 4 * d // dpn
    vmem = pl.BlockSpec(memory_space=pltpu.VMEM)
    dma = pltpu.SemaphoreType.DMA
    nz = dpn // 2
    moe, grad_tokens, router = pl.pallas_call(
        functools.partial(kernel, sizes),
        out_shape=(
            jax.ShapeDtypeStruct((t_count, d), BF16),
            jax.ShapeDtypeStruct((t_count, d), BF16),
            jax.ShapeDtypeStruct((32, d), F32),
        ),
        in_specs=[vmem] * 7,
        out_specs=(vmem,) * 3,
        scratch_shapes=[block] * 8
        + [
            pltpu.VMEM((groups * ROWS, ff), F32),
            pltpu.VMEM((groups * ROWS, ff), F32),
            pltpu.VMEM((dpn, 3, shard, ff), BF16),
            pltpu.VMEM((32, d), F32),
            pltpu.VMEM((dpn - 1, 8, wide), F32),
            pltpu.VMEM((cpn // 2, 8, wide), F32),
            pltpu.VMEM((2 * tpn, 8, wide), F32),
            pltpu.VMEM((dpn, 8, wide), F32),
            dma((4,)), dma((4,)), dma((4,)), dma((2,)),
            dma((nz - 1,)), dma((nz - 1,)), dma((nz,)), dma((nz,)),
            dma((4,)), dma((4,)),
        ],
        compiler_params=pltpu.CompilerParams(collective_id=0, has_side_effects=True),
        name="experts",
    )(tokens, expert_ids, router_weight, gate_weight, up_weight, down_weight, grad_out)
    return moe, grad_tokens, router[: router_weight.shape[1]].T


def solution(mesh):
    in_specs = (
        P(("dp", "tp", "cp"), None),
        P(("dp", "tp", "cp"), None),
        P(),
        P(("tp", "cp"), "dp", None),
        P(("tp", "cp"), "dp", None),
        P(("tp", "cp"), None, "dp"),
        P(("dp", "tp", "cp"), None),
    )
    out_specs = (P(("dp", "tp", "cp"), None), P(("dp", "tp", "cp"), None), P())
    return jax.shard_map(
        on_device, mesh=mesh, in_specs=in_specs, out_specs=out_specs, check_vma=False
    )
```

time: 454 us -> 104 us (0.23)
  waiting for transfers between devices: 282 us -> 0 us
  Pallas kernels: 0 us -> 96.7 us
  blocking collectives: 95.7 us -> 0 us
  starting transfers between devices: 26.3 us -> 0 us
  local copies, waits for them, and re-layouts: 20.4 us -> 6.48 us
  between operations: 14.4 us -> 0.66 us
  matrix products: 7.95 us -> 0 us
  other arithmetic: 7.16 us -> 0 us
    psum x1 -> x0, waiting for transfers between devices: 237 us -> none  [on_device(): router_grad = lax.psum(router_part, ('dp', 'tp', 'cp'))]
    pallas_call x0 -> x1, Pallas kernels: none -> 96.7 us  [on_device(): pl.pallas_call(functools.partial(kernel, sizes), out_shape=(jax.ShapeDtyp...]
    all_gather x3 -> x0, blocking collectives: 62 us -> none  [the longest x1 27.5 us: on_device(): lax.all_gather(down_weight[0], 'dp', axis=1, tiled=True)]
    all_to_all x3 -> x0, waiting for transfers between devices: 44.8 us -> none  [trade(): lax.all_to_all(shaped, ('tp', 'cp'), split_axis=1, concat_axis=1, tiled=T...]
    all_to_all x1 -> x0, blocking collectives: 33.6 us -> none  [trade(): lax.all_to_all(shaped, ('tp', 'cp'), split_axis=1, concat_axis=1, tiled=T...]
    all_to_all x3 -> x0, starting transfers between devices: 26.3 us -> none  [trade(): lax.all_to_all(shaped, ('tp', 'cp'), split_axis=1, concat_axis=1, tiled=T...]
    dot_general x10 -> x0, matrix products: 7.95 us -> none  [the longest x1 1.8 us: expert_backward(): lax.dot_general(received_grad, w_down, contract, preferred_element_type=j...]
    gather x7 -> x0, local copies, waits for them, and re-layouts: 4.78 us -> none  [the longest x5 2.44 us: on_device(): chosen = jnp.take_along_axis(logits, expert_ids, axis=1)]
  transfers between devices with their start and end apart: 4 -> 0, of which waited for: 3 -> 0; matrix products, arithmetic and copies ran while one was open for 3% -> 0% of each run, Pallas kernels for 0% -> 0%
where the time goes in v1:
time: 104 us
  Pallas kernels  96.7 us (93%)
  local copies, waits for them, and re-layouts  6.48 us (6%)
    pallas_call x1, Pallas kernels, on_device(): pl.pallas_call(functools.partial(kernel, sizes), out_shape=(jax.ShapeDtyp...  96.7 us
    unnamed x14, local copies, waits for them, and re-layouts  6.48 us

profile of v1, /device:TPU:1, one launch (start us, length us, event | category | flops | bytes accessed | tf_op | source)
XLA Modules:
  0.0 103.8 jit_solution(10434266561679824504)
XLA Ops:
  0.6 0.0 copy-start.3
  0.6 1.4 %copy.10.ids_ref = s32[128,2]{1,0:T(8,128)} copy(s32[128,2]{0,1:T(2,128)} %param.8) | data formatting | bytes 2048 | tf_op args[1]
  2.1 0.0 copy-done.3
  2.1 0.0 copy-start.2
  2.1 0.8 copy.12.wd_ref
  2.8 0.1 copy-done.2
  2.9 0.8 copy.11.rw_ref
  3.8 96.7 %experts.1 = (bf16[128,1024]{1,0:T(8,128)(2,1)}, bf16[128,1024]{1,0:T(8,128)(2,1)}, f32[32,1024]{1,0:T(8,128)}) custom-call(bf16[128,1024]{1,0:T(8,128)(2,1)} %tok_ref.1, s32[128,2]{1,0:T(8,128)} %copy.10.ids_ref, bf16[1024,32]{1,0:T(8,128)(2,1)} %copy.11.rw_ref, bf16[1,64,384]{2,1,0:T(8,128)(2,1)} %wg_ref.1, bf16[1,64,384]{2,1,0:T(8,128)(2,1)} %wu_ref.1, ...), custom_call_target="tpu_custom_call" | custom-call | tf_op jit(solution)/shard_map/experts/pallas_call | solution.py:370
  100.4 0.0 copy-start
  100.4 1.7 %copy.16 = bf16[128,1024]{1,0:T(8,128)(2,1)} copy(bf16[128,1024]{1,0:T(8,128)(2,1)} %get-tuple-element.12) | data formatting | bytes 524288
  102.2 0.0 copy-done
  102.2 0.0 copy-start.1
  102.2 0.7 copy.17
  102.9 0.3 copy-done.1
  103.2 0.7 copy.18
Async XLA Ops:
  0.6 1.4 %copy-start.3 = (bf16[1,384,64]{1,2,0:T(8,128)(2,1)S(1)}, bf16[1,384,64]{1,2,0:T(8,128)(2,1)}, u32[]{:S(2)}) copy-start(bf16[1,384,64]{1,2,0:T(8,128)(2,1)} %param.12) | copy-start | bytes 147460
  2.1 0.8 copy-start.2
  100.4 1.7 %copy-start = (bf16[128,1024]{1,0:T(8,128)(2,1)S(1)}, bf16[128,1024]{1,0:T(8,128)(2,1)}, u32[]{:S(2)}) copy-start(bf16[128,1024]{1,0:T(8,128)(2,1)} %get-tuple-element.13) | copy-start | bytes 786436
  102.2 1.0 copy-start.1

commit v2 on v1

--- a/solution.py
+++ b/solution.py
@@ -31,8 +31,8 @@
     sizes,
     tok_ref, ids_ref, rw_ref, wg_ref, wu_ref, wd_ref, g_ref,
     moe_ref, gt_ref, rg_ref,
-    sx, sg, rx, rg, px, pg, cx, cg, act, up, w, part, r1, ax, ay, fin,
-    s_in, r_in, s_out, r_out, s_ring, r_ring, s_pair, r_pair, s_ar, r_ar,
+    sx, sg, rx, rg, px, pg, cx, cg, act, up, ws, w, part, r1, ax, ay, fin,
+    s_in, r_in, s_out, r_out, s_ring, r_ring, s_far, s_pair, r_own, s_ar, r_ar,
 ):
     dpn, tpn, cpn = sizes
     groups = tpn * cpn
@@ -44,21 +44,35 @@
     dp = lax.axis_index("dp")
     tp = lax.axis_index("tp")
     cp = lax.axis_index("cp")
-    me = tp * cpn + cp
     xi = lax.rem(cp, nx)
     yh = cp // nx
+    yn = 2 * tpn
+    y = yh * tpn + tp
     z = dp // 2
     core = lax.rem(dp, 2)
-
-    def peer(r):
-        to_tp = lax.rem(tp + lax.rem(r // nx, tpn), tpn)
-        to_cp = lax.rem(yh + r // half, 2) * nx + lax.rem(xi + lax.rem(r, nx), nx)
-        return to_tp, to_cp
-
-    def mirror(r):
-        back_x = lax.rem(nx - lax.rem(r, nx), nx)
-        back_tp = lax.rem(tpn - lax.rem(r // nx, tpn), tpn)
-        return (r // half) * half + back_tp * nx + back_x
+    mine = tp * cpn + core * nx + xi
+
+    def shift(dl, h):
+        return dl - tpn * ((2 * dl + h) // (tpn + 1))
+
+    def split(r):
+        return r // (2 * nx), lax.rem(r // 2, nx), lax.rem(r, 2)
+
+    def device(to_y, to_x, to_core):
+        return z * 2 + to_core, lax.rem(to_y, tpn), (to_y // tpn) * nx + to_x
+
+    def host(r):
+        dl, dx, dc = split(r)
+        h = lax.rem(core + dc, 2)
+        to_x = lax.rem(xi + dx, nx)
+        expert = lax.rem(tp + dl, tpn) * cpn + h * nx + to_x
+        return expert, device(lax.rem(y + shift(dl, h) + yn, yn), to_x, h)
+
+    def home(r):
+        dl, dx, dc = split(r)
+        return device(
+            lax.rem(y - shift(dl, core) + yn, yn), lax.rem(xi - dx + nx, nx), lax.rem(core - dc + 2, 2)
+        )
 
     def remote(src, dst, send, recv, device):
         return pltpu.make_async_remote_copy(
@@ -71,19 +85,20 @@
 
     barrier = pltpu.get_barrier_semaphore()
 
+    def greet(to):
+        pl.semaphore_signal(barrier, inc=1, device_id=to, device_id_type=MESH)
+
     def greet_plane(r, carry):
-        to_tp, to_cp = peer(r)
-        pl.semaphore_signal(barrier, inc=1, device_id=(dp, to_tp, to_cp), device_id_type=MESH)
+        dy, rest = r // (2 * nx), lax.rem(r, 2 * nx)
+        greet(device(lax.rem(y + dy, yn), lax.rem(xi + rest // 2, nx), lax.rem(core + rest, 2)))
         return carry
 
     def greet_dp(o, carry):
-        pl.semaphore_signal(
-            barrier, inc=1, device_id=(lax.rem(dp + o, dpn), tp, cp), device_id_type=MESH
-        )
+        greet((lax.rem(z + o // 2, nz) * 2 + lax.rem(o, 2), tp, cp))
         return carry
 
-    lax.fori_loop(1, groups, greet_plane, 0)
-    lax.fori_loop(1, dpn, greet_dp, 0)
+    lax.fori_loop(1, 2 * groups, greet_plane, 0)
+    lax.fori_loop(2, dpn, greet_dp, 0)
 
     tokens = tok_ref[...]
     grads = g_ref[...]
@@ -116,43 +131,42 @@
 
     shard = wg_ref.shape[1]
     eye = (iota((shard, shard), 0) == iota((shard, shard), 1)).astype(BF16)
-    w[dp, 0] = wg_ref[0]
-    w[dp, 1] = wu_ref[0]
-    w[dp, 2] = mm_t(eye, wd_ref[0]).astype(BF16)
-
-    pl.semaphore_wait(barrier, groups - 1 + dpn - 1)
-
-    def ring(step, sign):
-        slot = lax.rem(z - sign * step + nz, nz) * 2 + core
-        index = step if sign > 0 else nz // 2 + step
+    shards = [wg_ref[0], wu_ref[0], mm_t(eye, wd_ref[0]).astype(BF16)]
+    for i in range(3):
+        ws[i] = shards[i]
+
+    @pl.when(core == yh)
+    def _():
+        for i in range(3):
+            w[i, dp] = shards[i]
+
+    pl.semaphore_wait(barrier, 2 * groups - 1 + dpn - 2)
+
+    def far(i):
         return remote(
-            w.at[slot], w.at[slot], s_ring.at[index], r_ring.at[index],
-            (lax.rem(z + sign + nz, nz) * 2 + core, tp, cp),
-        )
-
-    def pair(index, shift):
-        slot = lax.rem(z + shift + nz, nz) * 2 + core
+            ws.at[i], w.at[i, dp], s_far.at[i], r_own.at[i],
+            (z * 2 + yh, tp, (1 - yh) * nx + xi),
+        )
+
+    def pair(i):
         return remote(
-            w.at[slot], w.at[slot], s_pair.at[index], r_pair.at[index],
-            (z * 2 + 1 - core, tp, cp),
-        )
-
-    rights, lefts = nz // 2, nz // 2 - 1
-    right = [ring(s, 1) for s in range(rights)]
-    left = [ring(s, -1) for s in range(lefts)]
-    pairs = [pair(0, 0)]
-    right[0].start()
-    if lefts:
-        left[0].start()
-    pairs[0].start()
+            ws.at[i], w.at[i, dp], s_pair.at[i], r_own.at[i], (z * 2 + 1 - core, tp, cp)
+        )
+
+    for i in range(3):
+        far(i).start()
+
+    @pl.when(core != yh)
+    def _():
+        for i in range(3):
+            pair(i).start()
 
     def send_in(src, dst, phase):
         for h in range(2):
             def one(r, carry):
-                to_tp, to_cp = peer(r)
+                expert, to = host(r)
                 remote(
-                    src.at[to_tp * cpn + to_cp], dst.at[mirror(r)],
-                    s_in.at[2 * phase + h], r_in.at[2 * phase + h], (dp, to_tp, to_cp),
+                    src.at[expert], dst.at[r], s_in.at[2 * phase + h], r_in.at[2 * phase + h], to
                 ).start()
                 return carry
 
@@ -160,8 +174,38 @@
 
     send_in(sx, rx, 0)
     send_in(sg, rg, 1)
-    rx[0] = sx[me]
-    rg[0] = sg[me]
+    rx[0] = sx[mine]
+    rg[0] = sg[mine]
+
+    steps = nz // 2
+
+    def ring(sign, step, i):
+        at = pl.ds(lax.rem(z - sign * step + nz, nz) * 2, 2)
+        index = ((0 if sign > 0 else steps) + step) * 3 + i
+        return remote(
+            w.at[i, at], w.at[i, at], s_ring.at[index], r_ring.at[index],
+            (lax.rem(z + sign + nz, nz) * 2 + core, tp, cp),
+        )
+
+    links = {}
+    for sign in (1, -1):
+        for s in range(steps):
+            for i in range(3):
+                if s + 1 < steps or (i == 1) == (sign < 0):
+                    links[sign, s, i] = ring(sign, s, i)
+
+    for i in range(3):
+        @pl.when(core == yh)
+        def _():
+            wait_bytes(w.at[i, pl.ds(0, 1)], r_own.at[i])
+
+        @pl.when(core != yh)
+        def _():
+            wait_bytes(w.at[i, pl.ds(0, 2)], r_own.at[i])
+
+        for sign in (1, -1):
+            if (sign, 0, i) in links:
+                links[sign, 0, i].start()
 
     logits = mm(tokens, rw_ref[...])
     ecount = rw_ref.shape[1]
@@ -180,22 +224,13 @@
         named = mm(hot[k].astype(BF16), spread) > 0.5
         picks.append([choice(named, slot, row, None)] + [choice(named, slot, row, j) for j in range(3)])
 
-    for s in range(rights):
-        right[s].wait_recv()
-        if s + 1 < rights:
-            right[s + 1].start()
-        copy = pair(len(pairs), -(s + 1))
-        copy.start()
-        pairs.append(copy)
-        if s < lefts:
-            left[s].wait_recv()
-            if s + 1 < lefts:
-                left[s + 1].start()
-            copy = pair(len(pairs), s + 1)
-            copy.start()
-            pairs.append(copy)
-    for copy in pairs:
-        copy.wait_recv()
+    for s in range(steps):
+        for i in range(3):
+            for sign in (1, -1):
+                if (sign, s, i) in links:
+                    links[sign, s, i].wait_recv()
+                if (sign, s + 1, i) in links:
+                    links[sign, s + 1, i].start()
 
     size = half * ROWS
     pr, qr = iota((size, size), 0), iota((size, size), 1)
@@ -224,7 +259,7 @@
             )
 
     def weight(i):
-        return w[:, i].reshape(d, w.shape[3])
+        return w[i].reshape(d, w.shape[3])
 
     def wait_in(ref, phase, h):
         lo = max(1, half * h)
@@ -232,10 +267,8 @@
 
     def send_out(src, dst, phase, h):
         def one(r, carry):
-            to_tp, to_cp = peer(r)
             remote(
-                src.at[r], dst.at[me], s_out.at[2 * phase + h], r_out.at[phase],
-                (dp, to_tp, to_cp),
+                src.at[r], dst.at[mine], s_out.at[2 * phase + h], r_out.at[phase], home(r)
             ).start()
             return carry
 
@@ -251,7 +284,7 @@
         hidden = (gate * jax.nn.sigmoid(gate) * upper_act).astype(BF16)
         close_rows(mm_t(hidden, weight(2)).astype(BF16), px, h)
         send_out(px, cx, 0, h)
-    cx[me] = px[0]
+    cx[mine] = px[0]
     for h in range(2):
         wait_in(rg, 1, h)
         rows = open_rows(rg, h)
@@ -264,7 +297,7 @@
         back = mm_t(grad_gate, weight(0)) + mm_t(grad_up, weight(1))
         close_rows(back.astype(BF16), pg, h)
         send_out(pg, cg, 1, h)
-    cg[me] = pg[0]
+    cg[mine] = pg[0]
 
     def home_rows(ref, k):
         packed = ref[...].reshape(span, 3 * q)
@@ -312,13 +345,11 @@
             (dp, tp, yh * nx + lax.rem(xi + o, nx)),
         ).start()
     wait_bytes(ax.at[pl.ds(0, nx - 1)], r_ar.at[1])
-    yn = 2 * tpn
-    yi = yh * tpn + tp
-    ay[yi] = jnp.sum(ax[...], axis=0)
+    ay[y] = jnp.sum(ax[...], axis=0)
     for o in range(1, yn):
-        to = lax.rem(yi + o, yn)
+        to = lax.rem(y + o, yn)
         remote(
-            ay.at[yi], ay.at[yi], s_ar.at[2], r_ar.at[2],
+            ay.at[y], ay.at[y], s_ar.at[2], r_ar.at[2],
             (dp, lax.rem(to, tpn), (to // tpn) * nx + xi),
         ).start()
     wait_bytes(ay.at[pl.ds(0, yn - 1)], r_ar.at[2])
@@ -348,7 +379,15 @@
         for h in range(2):
             lo = max(1, half * h)
             wait_bytes(ref.at[pl.ds(lo, half * (h + 1) - lo)], s_out.at[2 * phase + h])
-    for copy in right + left + pairs:
+    for i in range(3):
+        far(i).wait_send()
+
+    @pl.when(core != yh)
+    def _():
+        for i in range(3):
+            pair(i).wait_send()
+
+    for copy in links.values():
         copy.wait_send()
     wait_bytes(r1, s_ar.at[0])
     wait_bytes(ax.at[pl.ds(0, nx - 1)], s_ar.at[1])
@@ -380,14 +419,15 @@
         + [
             pltpu.VMEM((groups * ROWS, ff), F32),
             pltpu.VMEM((groups * ROWS, ff), F32),
-            pltpu.VMEM((dpn, 3, shard, ff), BF16),
+            pltpu.VMEM((3, shard, ff), BF16),
+            pltpu.VMEM((3, dpn, shard, ff), BF16),
             pltpu.VMEM((32, d), F32),
             pltpu.VMEM((dpn - 1, 8, wide), F32),
             pltpu.VMEM((cpn // 2, 8, wide), F32),
             pltpu.VMEM((2 * tpn, 8, wide), F32),
             pltpu.VMEM((dpn, 8, wide), F32),
             dma((4,)), dma((4,)), dma((4,)), dma((2,)),
-            dma((nz - 1,)), dma((nz - 1,)), dma((nz,)), dma((nz,)),
+            dma((3 * nz,)), dma((3 * nz,)), dma((3,)), dma((3,)), dma((3,)),
             dma((4,)), dma((4,)),
         ],
         compiler_params=pltpu.CompilerParams(collective_id=0, has_side_effects=True),

time: 104 us -> 92.9 us (0.89)
  Pallas kernels: 96.7 us -> 85.5 us
    pallas_call x1, Pallas kernels: 96.7 us -> 85.5 us  [on_device(): pl.pallas_call(functools.partial(kernel, sizes), out_shape=(jax.ShapeDtyp...]
where the time goes in v2:
time: 92.9 us; the launch traced here: 92.7 us
  Pallas kernels  85.5 us (92%)
  local copies, waits for them, and re-layouts  6.48 us (7%)
    pallas_call x1, Pallas kernels, on_device(): pl.pallas_call(functools.partial(kernel, sizes), out_shape=(jax.ShapeDtyp...  85.5 us
    unnamed x14, local copies, waits for them, and re-layouts  6.48 us

profile of v2, /device:TPU:1, one launch (start us, length us, event | category | flops | bytes accessed | tf_op | source)
XLA Modules:
  0.0 92.7 jit_solution(13697420257620610420)
XLA Ops:
  0.6 0.0 copy-start.3
  0.6 1.4 %copy.10.ids_ref = s32[128,2]{1,0:T(8,128)} copy(s32[128,2]{0,1:T(2,128)} %param.8) | data formatting | bytes 2048 | tf_op args[1]
  2.1 0.0 copy-done.3
  2.1 0.0 copy-start.2
  2.1 0.8 copy.12.wd_ref
  2.8 0.1 copy-done.2
  2.9 0.8 copy.11.rw_ref
  3.8 85.5 %experts.1 = (bf16[128,1024]{1,0:T(8,128)(2,1)}, bf16[128,1024]{1,0:T(8,128)(2,1)}, f32[32,1024]{1,0:T(8,128)}) custom-call(bf16[128,1024]{1,0:T(8,128)(2,1)} %tok_ref.1, s32[128,2]{1,0:T(8,128)} %copy.10.ids_ref, bf16[1024,32]{1,0:T(8,128)(2,1)} %copy.11.rw_ref, bf16[1,64,384]{2,1,0:T(8,128)(2,1)} %wg_ref.1, bf16[1,64,384]{2,1,0:T(8,128)(2,1)} %wu_ref.1, ...), custom_call_target="tpu_custom_call" | custom-call | tf_op jit(solution)/shard_map/experts/pallas_call | solution.py:409
  89.3 0.0 copy-start
  89.3 1.7 %copy.16 = bf16[128,1024]{1,0:T(8,128)(2,1)} copy(bf16[128,1024]{1,0:T(8,128)(2,1)} %get-tuple-element.12) | data formatting | bytes 524288
  91.0 0.0 copy-done
  91.0 0.0 copy-start.1
  91.0 0.7 copy.17
  91.7 0.3 copy-done.1
  92.0 0.7 copy.18
Async XLA Ops:
  0.6 1.4 %copy-start.3 = (bf16[1,384,64]{1,2,0:T(8,128)(2,1)S(1)}, bf16[1,384,64]{1,2,0:T(8,128)(2,1)}, u32[]{:S(2)}) copy-start(bf16[1,384,64]{1,2,0:T(8,128)(2,1)} %param.12) | copy-start | bytes 147460
  2.1 0.8 copy-start.2
  89.3 1.7 %copy-start = (bf16[128,1024]{1,0:T(8,128)(2,1)S(1)}, bf16[128,1024]{1,0:T(8,128)(2,1)}, u32[]{:S(2)}) copy-start(bf16[128,1024]{1,0:T(8,128)(2,1)} %get-tuple-element.13) | copy-start | bytes 786436
  91.0 1.0 %copy-start.1 = (f32[32,1024]{1,0:T(8,128)S(1)}, f32[32,1024]{1,0:T(8,128)}, u32[]{:S(2)}) copy-start(f32[32,1024]{1,0:T(8,128)} %get-tuple-element.8) | copy-start | bytes 393220

commit v3 on v2

--- a/solution.py
+++ b/solution.py
@@ -31,7 +31,7 @@
     sizes,
     tok_ref, ids_ref, rw_ref, wg_ref, wu_ref, wd_ref, g_ref,
     moe_ref, gt_ref, rg_ref,
-    sx, sg, rx, rg, px, pg, cx, cg, act, up, ws, w, part, r1, ax, ay, fin,
+    sx, sg, rx, rg, px, pg, cx, cg, xs, gs, act, up, ws, w, part, r1, ax, ay, fin,
     s_in, r_in, s_out, r_out, s_ring, r_ring, s_far, s_pair, r_own, s_ar, r_ar,
 ):
     dpn, tpn, cpn = sizes
@@ -100,12 +100,20 @@
     lax.fori_loop(1, 2 * groups, greet_plane, 0)
     lax.fori_loop(2, dpn, greet_dp, 0)
 
+    shards = [wg_ref[0], wu_ref[0], wd_ref[0]]
+    for i in range(3):
+        ws[i] = shards[i]
+
+    @pl.when(core == yh)
+    def _():
+        for i in range(3):
+            w[i, dp] = shards[i]
+
     tokens = tok_ref[...]
     grads = g_ref[...]
-    lane = iota((t_count, LANES), 1)
-    hot = [(lane == ids_ref[:, k : k + 1]).astype(F32) for k in range(2)]
-    both = hot[0] + hot[1]
-    both_t = both.T.astype(BF16)
+    expert = iota((LANES, t_count), 0)
+    hot_t = [(expert == ids_ref[k : k + 1, :]).astype(F32) for k in range(2)]
+    both_t = (hot_t[0] + hot_t[1]).astype(BF16)
     upper = (iota((t_count, t_count), 0) < iota((t_count, t_count), 1)).astype(BF16)
     before_t = mm(both_t, upper).astype(BF16)
     span = groups * ROWS
@@ -127,18 +135,6 @@
             out[:, :, q * j : q * (j + 1)] = piece.astype(BF16).reshape(groups, ROWS, q)
 
     pack_home(tokens, sx)
-    pack_home(grads, sg)
-
-    shard = wg_ref.shape[1]
-    eye = (iota((shard, shard), 0) == iota((shard, shard), 1)).astype(BF16)
-    shards = [wg_ref[0], wu_ref[0], mm_t(eye, wd_ref[0]).astype(BF16)]
-    for i in range(3):
-        ws[i] = shards[i]
-
-    @pl.when(core == yh)
-    def _():
-        for i in range(3):
-            w[i, dp] = shards[i]
 
     pl.semaphore_wait(barrier, 2 * groups - 1 + dpn - 2)
 
@@ -160,6 +156,37 @@
     def _():
         for i in range(3):
             pair(i).start()
+
+    steps = nz // 2
+
+    def ring(sign, step, i):
+        at = pl.ds(lax.rem(z - sign * step + nz, nz) * 2, 2)
+        index = ((0 if sign > 0 else steps) + step) * 3 + i
+        return remote(
+            w.at[i, at], w.at[i, at], s_ring.at[index], r_ring.at[index],
+            (lax.rem(z + sign + nz, nz) * 2 + core, tp, cp),
+        )
+
+    links = {}
+    for sign in (1, -1):
+        for s in range(steps):
+            for i in range(3):
+                if s + 1 < steps or (i == 1) == (sign < 0):
+                    links[sign, s, i] = ring(sign, s, i)
+
+    def enter_ring():
+        for i in range(3):
+            for sign in (1, -1):
+                if (sign, 0, i) in links:
+                    links[sign, 0, i].start()
+
+    def ring_step(s, chunks=(0, 1, 2)):
+        for i in chunks:
+            for sign in (1, -1):
+                if (sign, s, i) in links:
+                    links[sign, s, i].wait_recv()
+                if (sign, s + 1, i) in links:
+                    links[sign, s + 1, i].start()
 
     def send_in(src, dst, phase):
         for h in range(2):
@@ -173,47 +200,35 @@
             lax.fori_loop(max(1, half * h), half * (h + 1), one, 0)
 
     send_in(sx, rx, 0)
+
+    @pl.when(core == yh)
+    def _():
+        for i in range(3):
+            wait_bytes(w.at[i, pl.ds(0, 1)], r_own.at[i])
+        enter_ring()
+
+    pack_home(grads, sg)
     send_in(sg, rg, 1)
     rx[0] = sx[mine]
     rg[0] = sg[mine]
 
-    steps = nz // 2
-
-    def ring(sign, step, i):
-        at = pl.ds(lax.rem(z - sign * step + nz, nz) * 2, 2)
-        index = ((0 if sign > 0 else steps) + step) * 3 + i
-        return remote(
-            w.at[i, at], w.at[i, at], s_ring.at[index], r_ring.at[index],
-            (lax.rem(z + sign + nz, nz) * 2 + core, tp, cp),
-        )
-
-    links = {}
-    for sign in (1, -1):
-        for s in range(steps):
-            for i in range(3):
-                if s + 1 < steps or (i == 1) == (sign < 0):
-                    links[sign, s, i] = ring(sign, s, i)
-
-    for i in range(3):
-        @pl.when(core == yh)
-        def _():
-            wait_bytes(w.at[i, pl.ds(0, 1)], r_own.at[i])
-
-        @pl.when(core != yh)
-        def _():
+    @pl.when(core != yh)
+    def _():
+        for i in range(3):
             wait_bytes(w.at[i, pl.ds(0, 2)], r_own.at[i])
-
-        for sign in (1, -1):
-            if (sign, 0, i) in links:
-                links[sign, 0, i].start()
-
-    logits = mm(tokens, rw_ref[...])
-    ecount = rw_ref.shape[1]
+        enter_ring()
+
+    logits = mm_t(tokens, rw_ref[...])
+    ecount = rw_ref.shape[0]
+    hot = [hot_t[k].T for k in range(2)]
+    both = hot[0] + hot[1]
     chosen = [jnp.sum(logits * hot[k][:, :ecount], axis=1, keepdims=True) for k in range(2)]
     mixing = [
         1.0 / (1.0 + jnp.exp(chosen[1] - chosen[0])),
         1.0 / (1.0 + jnp.exp(chosen[0] - chosen[1])),
     ]
+    if steps > 1:
+        ring_step(0)
     lower = (iota((t_count, t_count), 1) < iota((t_count, t_count), 0)).astype(BF16)
     before = mm(lower, both.astype(BF16)).astype(BF16)
     spread = (iota((LANES, span), 1) // ROWS == iota((LANES, span), 0)).astype(BF16)
@@ -223,14 +238,8 @@
     for k in range(2):
         named = mm(hot[k].astype(BF16), spread) > 0.5
         picks.append([choice(named, slot, row, None)] + [choice(named, slot, row, j) for j in range(3)])
-
-    for s in range(steps):
-        for i in range(3):
-            for sign in (1, -1):
-                if (sign, s, i) in links:
-                    links[sign, s, i].wait_recv()
-                if (sign, s + 1, i) in links:
-                    links[sign, s + 1, i].start()
+    for s in range(1, steps - 1):
+        ring_step(s)
 
     size = half * ROWS
     pr, qr = iota((size, size), 0), iota((size, size), 1)
@@ -276,21 +285,28 @@
 
     for h in range(2):
         wait_in(rx, 0, h)
-        rows = open_rows(rx, h)
-        gate = mm(rows, weight(0))
-        upper_act = mm(rows, weight(1))
-        act[size * h : size * (h + 1)] = gate
-        up[size * h : size * (h + 1)] = upper_act
-        hidden = (gate * jax.nn.sigmoid(gate) * upper_act).astype(BF16)
+        xs[size * h : size * (h + 1)] = open_rows(rx, h)
+    for h in range(2):
+        wait_in(rg, 1, h)
+        gs[size * h : size * (h + 1)] = open_rows(rg, h)
+    ring_step(steps - 1, (0, 1))
+    for h in range(2):
+        at = slice(size * h, size * (h + 1))
+        act[at] = mm(xs[at], weight(0))
+        up[at] = mm(xs[at], weight(1))
+    ring_step(steps - 1, (2,))
+    for h in range(2):
+        at = slice(size * h, size * (h + 1))
+        gate = act[at]
+        hidden = (gate * jax.nn.sigmoid(gate) * up[at]).astype(BF16)
         close_rows(mm_t(hidden, weight(2)).astype(BF16), px, h)
         send_out(px, cx, 0, h)
     cx[mine] = px[0]
     for h in range(2):
-        wait_in(rg, 1, h)
-        rows = open_rows(rg, h)
-        grad_hidden = mm(rows, weight(2))
-        gate = act[size * h : size * (h + 1)]
-        upper_act = up[size * h : size * (h + 1)]
+        at = slice(size * h, size * (h + 1))
+        grad_hidden = mm(gs[at], weight(2))
+        gate = act[at]
+        upper_act = up[at]
         sigma = jax.nn.sigmoid(gate)
         grad_gate = (grad_hidden * upper_act * sigma * (1.0 + gate * (1.0 - sigma))).astype(BF16)
         grad_up = (grad_hidden * gate * sigma).astype(BF16)
@@ -334,7 +350,7 @@
 
     lax.fori_loop(1, dpn, scatter, 0)
 
-    router_back = mm_t(dense.astype(BF16)[:, :ecount], rw_ref[...])
+    router_back = mm(dense.astype(BF16)[:, :ecount], rw_ref[...])
 
     wait_bytes(r1, r_ar.at[0])
     rows_own, cols_own = chunk(dp)
@@ -417,6 +433,8 @@
         out_specs=(vmem,) * 3,
         scratch_shapes=[block] * 8
         + [
+            pltpu.VMEM((groups * ROWS, d), BF16),
+            pltpu.VMEM((groups * ROWS, d), BF16),
             pltpu.VMEM((groups * ROWS, ff), F32),
             pltpu.VMEM((groups * ROWS, ff), F32),
             pltpu.VMEM((3, shard, ff), BF16),
@@ -432,7 +450,10 @@
         ],
         compiler_params=pltpu.CompilerParams(collective_id=0, has_side_effects=True),
         name="experts",
-    )(tokens, expert_ids, router_weight, gate_weight, up_weight, down_weight, grad_out)
+    )(
+        tokens, expert_ids.T, router_weight.T, gate_weight, up_weight,
+        jnp.swapaxes(down_weight, 1, 2), grad_out,
+    )
     return moe, grad_tokens, router[: router_weight.shape[1]].T
 
 

time: 92.9 us -> 91.8 us (0.988)
  local copies, waits for them, and re-layouts: 6.48 us -> 3.37 us
  Pallas kernels: 85.5 us -> 87.6 us
    unnamed x14 -> x7, local copies, waits for them, and re-layouts: 6.48 us -> 3.37 us
    pallas_call x1, Pallas kernels: 85.5 us -> 87.6 us  [on_device(): pl.pallas_call(functools.partial(kernel, sizes), out_shape=(jax.ShapeDtyp...]
where the time goes in v3:
time: 91.8 us; the launch traced here: 91.6 us
  Pallas kernels  87.6 us (95%)
  local copies, waits for them, and re-layouts  3.37 us (4%)
    pallas_call x1, Pallas kernels, on_device(): pl.pallas_call(functools.partial(kernel, sizes), out_shape=(jax.ShapeDtyp...  87.6 us
    unnamed x7, local copies, waits for them, and re-layouts  3.37 us

profile of v3, /device:TPU:1, one launch (start us, length us, event | category | flops | bytes accessed | tf_op | source)
XLA Modules:
  0.0 91.6 jit_solution(8081460576145940384)
XLA Ops:
  0.6 87.6 %experts.1 = (bf16[128,1024]{1,0:T(8,128)(2,1)}, bf16[128,1024]{1,0:T(8,128)(2,1)}, f32[32,1024]{1,0:T(8,128)}) custom-call(bf16[128,1024]{1,0:T(8,128)(2,1)} %tok_ref.1, s32[2,128]{1,0:T(2,128)} %bitcast.7, bf16[32,1024]{1,0:T(8,128)(2,1)} %bitcast.5, bf16[1,64,384]{2,1,0:T(8,128)(2,1)} %wg_ref.1, bf16[1,64,384]{2,1,0:T(8,128)(2,1)} %wu_ref.1, ...), custom_call_target="tpu_custom_call" | custom-call | tf_op jit(solution)/shard_map/experts/pallas_call | solution.py:425
  88.2 0.0 copy-start
  88.2 1.7 %copy.13 = bf16[128,1024]{1,0:T(8,128)(2,1)} copy(bf16[128,1024]{1,0:T(8,128)(2,1)} %get-tuple-element.12) | data formatting | bytes 524288
  89.9 0.0 copy-done
  89.9 0.0 copy-start.1
  89.9 0.7 copy.14
  90.6 0.3 copy-done.1
  90.9 0.7 copy.15
Async XLA Ops:
  88.2 1.7 %copy-start = (bf16[128,1024]{1,0:T(8,128)(2,1)S(1)}, bf16[128,1024]{1,0:T(8,128)(2,1)}, u32[]{:S(2)}) copy-start(bf16[128,1024]{1,0:T(8,128)(2,1)} %get-tuple-element.13) | copy-start | bytes 786436
  89.9 1.0 %copy-start.1 = (f32[32,1024]{1,0:T(8,128)S(1)}, f32[32,1024]{1,0:T(8,128)}, u32[]{:S(2)}) copy-start(f32[32,1024]{1,0:T(8,128)} %get-tuple-element.8) | copy-start | bytes 393220

commit v4 on v3

--- a/solution.py
+++ b/solution.py
@@ -31,7 +31,7 @@
     sizes,
     tok_ref, ids_ref, rw_ref, wg_ref, wu_ref, wd_ref, g_ref,
     moe_ref, gt_ref, rg_ref,
-    sx, sg, rx, rg, px, pg, cx, cg, xs, gs, act, up, ws, w, part, r1, ax, ay, fin,
+    sx, sg, rx, rg, px, pg, cx, cg, xs, gs, act, up, gh, so, si, ws, w, part, r1, ax, ay, fin,
     s_in, r_in, s_out, r_out, s_ring, r_ring, s_far, s_pair, r_own, s_ar, r_ar,
 ):
     dpn, tpn, cpn = sizes
@@ -55,24 +55,52 @@
     def shift(dl, h):
         return dl - tpn * ((2 * dl + h) // (tpn + 1))
 
-    def split(r):
-        return r // (2 * nx), lax.rem(r // 2, nx), lax.rem(r, 2)
-
-    def device(to_y, to_x, to_core):
-        return z * 2 + to_core, lax.rem(to_y, tpn), (to_y // tpn) * nx + to_x
-
-    def host(r):
-        dl, dx, dc = split(r)
-        h = lax.rem(core + dc, 2)
-        to_x = lax.rem(xi + dx, nx)
-        expert = lax.rem(tp + dl, tpn) * cpn + h * nx + to_x
-        return expert, device(lax.rem(y + shift(dl, h) + yn, yn), to_x, h)
-
-    def home(r):
-        dl, dx, dc = split(r)
-        return device(
-            lax.rem(y - shift(dl, core) + yn, yn), lax.rem(xi - dx + nx, nx), lax.rem(core - dc + 2, 2)
-        )
+    xs_up = [lax.rem(xi + dx, nx) for dx in range(nx)]
+    xs_down = [lax.rem(xi - dx + nx, nx) for dx in range(nx)]
+    cores = [core, 1 - core]
+
+    def column(to_y):
+        return lax.rem(to_y, tpn), (to_y // tpn) * nx
+
+    def each_host(h, fn):
+        def run(dl, carry):
+            to = [column(lax.rem(y + shift(dl, c) + yn, yn)) for c in range(2)]
+            first = [
+                (core * to[1 - dc][0] + (1 - core) * to[dc][0], core * to[1 - dc][1] + (1 - core) * to[dc][1])
+                for dc in range(2)
+            ]
+            for j in range(2 * nx):
+                dx, dc = j // 2, j % 2
+                to_tp, base = first[dc]
+
+                def send():
+                    expert = to_tp * cpn + cores[dc] * nx + xs_up[dx]
+                    fn(dl * (2 * nx) + j, expert, (z * 2 + cores[dc], to_tp, base + xs_up[dx]))
+
+                if j:
+                    send()
+                else:
+                    pl.when(dl > 0)(send)
+            return carry
+
+        lax.fori_loop(tpn // 2 * h, tpn // 2 * (h + 1), run, 0)
+
+    def each_home(h, fn):
+        def run(dl, carry):
+            to_tp, base = column(lax.rem(y - shift(dl, core) + yn, yn))
+            for j in range(2 * nx):
+                dx, dc = j // 2, j % 2
+
+                def send():
+                    fn(dl * (2 * nx) + j, (z * 2 + cores[dc], to_tp, base + xs_down[dx]))
+
+                if j:
+                    send()
+                else:
+                    pl.when(dl > 0)(send)
+            return carry
+
+        lax.fori_loop(tpn // 2 * h, tpn // 2 * (h + 1), run, 0)
 
     def remote(src, dst, send, recv, device):
         return pltpu.make_async_remote_copy(
@@ -88,17 +116,16 @@
     def greet(to):
         pl.semaphore_signal(barrier, inc=1, device_id=to, device_id_type=MESH)
 
-    def greet_plane(r, carry):
-        dy, rest = r // (2 * nx), lax.rem(r, 2 * nx)
-        greet(device(lax.rem(y + dy, yn), lax.rem(xi + rest // 2, nx), lax.rem(core + rest, 2)))
+    def greet_plane(to_tp, carry):
+        for to_cp in range(cpn):
+            for c in range(2):
+                other = (to_tp != tp) | (cp != to_cp) | (core != c)
+                pl.when(other)(functools.partial(greet, (z * 2 + c, to_tp, to_cp)))
         return carry
 
-    def greet_dp(o, carry):
-        greet((lax.rem(z + o // 2, nz) * 2 + lax.rem(o, 2), tp, cp))
-        return carry
-
-    lax.fori_loop(1, 2 * groups, greet_plane, 0)
-    lax.fori_loop(2, dpn, greet_dp, 0)
+    lax.fori_loop(0, tpn, greet_plane, 0)
+    for to in range(dpn):
+        pl.when(z != to // 2)(functools.partial(greet, (to, tp, cp)))
 
     shards = [wg_ref[0], wu_ref[0], wd_ref[0]]
     for i in range(3):
@@ -190,14 +217,10 @@
 
     def send_in(src, dst, phase):
         for h in range(2):
-            def one(r, carry):
-                expert, to = host(r)
-                remote(
-                    src.at[expert], dst.at[r], s_in.at[2 * phase + h], r_in.at[2 * phase + h], to
-                ).start()
-                return carry
-
-            lax.fori_loop(max(1, half * h), half * (h + 1), one, 0)
+            index = 2 * phase + h
+            each_host(h, lambda r, expert, to: remote(
+                src.at[expert], dst.at[r], s_in.at[index], r_in.at[index], to
+            ).start())
 
     send_in(sx, rx, 0)
 
@@ -234,6 +257,7 @@
     spread = (iota((LANES, span), 1) // ROWS == iota((LANES, span), 0)).astype(BF16)
     slot = mm(before, spread)
     row = lax.rem(iota((t_count, span), 1), ROWS)
+    slots = [jnp.sum(before.astype(F32) * hot[k], axis=1, keepdims=True) for k in range(2)]
     picks = []
     for k in range(2):
         named = mm(hot[k].astype(BF16), spread) > 0.5
@@ -275,13 +299,10 @@
         wait_bytes(ref.at[pl.ds(lo, half * (h + 1) - lo)], r_in.at[2 * phase + h])
 
     def send_out(src, dst, phase, h):
-        def one(r, carry):
-            remote(
-                src.at[r], dst.at[mine], s_out.at[2 * phase + h], r_out.at[phase], home(r)
-            ).start()
-            return carry
-
-        lax.fori_loop(max(1, half * h), half * (h + 1), one, 0)
+        index = 2 * phase + h
+        each_home(h, lambda r, to: remote(
+            src.at[r], dst.at[mine], s_out.at[index], r_out.at[phase], to
+        ).start())
 
     for h in range(2):
         wait_in(rx, 0, h)
@@ -295,24 +316,34 @@
         act[at] = mm(xs[at], weight(0))
         up[at] = mm(xs[at], weight(1))
     ring_step(steps - 1, (2,))
+    hiddens = []
+    lanes = iota((size, LANES), 1)
+    own_lane = lanes == lax.rem(iota((size, LANES), 0), ROWS)
     for h in range(2):
         at = slice(size * h, size * (h + 1))
         gate = act[at]
         hidden = (gate * jax.nn.sigmoid(gate) * up[at]).astype(BF16)
-        close_rows(mm_t(hidden, weight(2)).astype(BF16), px, h)
+        hiddens.append(hidden)
+        grad_hidden = mm(gs[at], weight(2))
+        gh[at] = grad_hidden
+        score = jnp.sum(hidden.astype(F32) * grad_hidden, axis=1, keepdims=True)
+        table = jnp.where(own_lane, score, 0.0).reshape(half, ROWS, LANES)
+        so[half * h : half * (h + 1)] = jnp.sum(table, axis=1, keepdims=True)
+    for h in range(2):
+        each_home(h, lambda r, to: remote(so.at[r], si.at[mine], s_ar.at[4], r_ar.at[4], to).start())
+    si[mine] = so[0]
+    for h in range(2):
+        close_rows(mm_t(hiddens[h], weight(2)).astype(BF16), px, h)
         send_out(px, cx, 0, h)
     cx[mine] = px[0]
     for h in range(2):
         at = slice(size * h, size * (h + 1))
-        grad_hidden = mm(gs[at], weight(2))
-        gate = act[at]
-        upper_act = up[at]
+        grad_hidden, gate, upper_act = gh[at], act[at], up[at]
         sigma = jax.nn.sigmoid(gate)
         grad_gate = (grad_hidden * upper_act * sigma * (1.0 + gate * (1.0 - sigma))).astype(BF16)
         grad_up = (grad_hidden * gate * sigma).astype(BF16)
         back = mm_t(grad_gate, weight(0)) + mm_t(grad_up, weight(1))
         close_rows(back.astype(BF16), pg, h)
-        send_out(pg, cg, 1, h)
     cg[mine] = pg[0]
 
     def home_rows(ref, k):
@@ -321,15 +352,20 @@
         tail = sum(mm(picks[k][1 + j], packed[:, q * j : q * (j + 1)]) for j in range(3))
         return jnp.concatenate([main, tail], axis=1)
 
-    wait_bytes(cx.at[pl.ds(0, groups - 1)], r_out.at[0])
-    grads32 = grads.astype(F32)
-    total = None
+    wait_bytes(si.at[pl.ds(0, groups - 1)], r_ar.at[4])
+    rest = si[...].reshape(groups, LANES)
+    pieces = []
+    for _ in range(3):
+        pieces.append(rest.astype(BF16))
+        rest = rest - pieces[-1].astype(F32)
+    token_lane = iota((t_count, LANES), 1).astype(F32)
     scores = []
     for k in range(2):
-        rows = home_rows(cx, k)
-        scores.append(jnp.sum(grads32 * rows, axis=1, keepdims=True))
-        total = mixing[k] * rows if total is None else total + mixing[k] * rows
-    moe_ref[...] = total.astype(BF16)
+        of_expert = hot[k][:, :groups].astype(BF16)
+        found = sum(mm(of_expert, piece) for piece in pieces)
+        scores.append(
+            jnp.sum(jnp.where(token_lane == slots[k], found, 0.0), axis=1, keepdims=True)
+        )
     mean = mixing[0] * scores[0] + mixing[1] * scores[1]
     dense = sum(hot[k] * (mixing[k] * (scores[k] - mean)) for k in range(2))
     dense_t = dense.T.astype(BF16)
@@ -339,44 +375,46 @@
     nb = d // cw
 
     def chunk(c):
-        return pl.ds(pl.multiple_of(8 * (c // nb), 8), 8), pl.ds(
-            pl.multiple_of(cw * lax.rem(c, nb), LANES), cw
-        )
-
-    def scatter(o, carry):
-        to = lax.rem(dp + o, dpn)
-        remote(part.at[chunk(to)], r1.at[o - 1], s_ar.at[0], r_ar.at[0], (to, tp, cp)).start()
-        return carry
-
-    lax.fori_loop(1, dpn, scatter, 0)
+        return slice(8 * (c // nb), 8 * (c // nb) + 8), slice(cw * (c % nb), cw * (c % nb + 1))
+
+    for to in range(dpn):
+        rows_to, cols_to = chunk(to)
+
+        @pl.when(dp != to)
+        def _():
+            remote(
+                part.at[rows_to, cols_to], r1.at[dp], s_ar.at[0], r_ar.at[0], (to, tp, cp)
+            ).start()
+
+        @pl.when(dp == to)
+        def _():
+            r1[dp] = part[rows_to, cols_to]
 
     router_back = mm(dense.astype(BF16)[:, :ecount], rw_ref[...])
 
-    wait_bytes(r1, r_ar.at[0])
-    rows_own, cols_own = chunk(dp)
-    ax[xi] = jnp.sum(r1[...], axis=0) + part[rows_own, cols_own]
+    wait_bytes(r1.at[pl.ds(0, dpn - 1)], r_ar.at[0])
+    ax[xi] = jnp.sum(r1[...], axis=0)
     for o in range(1, nx):
         remote(
-            ax.at[xi], ax.at[xi], s_ar.at[1], r_ar.at[1],
-            (dp, tp, yh * nx + lax.rem(xi + o, nx)),
+            ax.at[xi], ax.at[xi], s_ar.at[1], r_ar.at[1], (dp, tp, yh * nx + xs_up[o])
         ).start()
+    send_out(pg, cg, 1, 0)
     wait_bytes(ax.at[pl.ds(0, nx - 1)], r_ar.at[1])
     ay[y] = jnp.sum(ax[...], axis=0)
     for o in range(1, yn):
-        to = lax.rem(y + o, yn)
-        remote(
-            ay.at[y], ay.at[y], s_ar.at[2], r_ar.at[2],
-            (dp, lax.rem(to, tpn), (to // tpn) * nx + xi),
-        ).start()
+        to_tp, base = column(lax.rem(y + o, yn))
+        remote(ay.at[y], ay.at[y], s_ar.at[2], r_ar.at[2], (dp, to_tp, base + xi)).start()
+    send_out(pg, cg, 1, 1)
+
+    wait_bytes(cx.at[pl.ds(0, groups - 1)], r_out.at[0])
+    moe_ref[...] = (mixing[0] * home_rows(cx, 0) + mixing[1] * home_rows(cx, 1)).astype(BF16)
+
     wait_bytes(ay.at[pl.ds(0, yn - 1)], r_ar.at[2])
     fin[dp] = jnp.sum(ay[...], axis=0)
-
-    def gather(o, carry):
-        to = lax.rem(dp + o, dpn)
-        remote(fin.at[dp], fin.at[dp], s_ar.at[3], r_ar.at[3], (to, tp, cp)).start()
-        return carry
-
-    lax.fori_loop(1, dpn, gather, 0)
+    for to in range(dpn):
+        @pl.when(dp != to)
+        def _():
+            remote(fin.at[dp], fin.at[dp], s_ar.at[3], r_ar.at[3], (to, tp, cp)).start()
 
     wait_bytes(cg.at[pl.ds(0, groups - 1)], r_out.at[1])
     gt_ref[...] = (
@@ -385,7 +423,7 @@
 
     wait_bytes(fin.at[pl.ds(0, dpn - 1)], r_ar.at[3])
     for c in range(dpn):
-        rg_ref[8 * (c // nb) : 8 * (c // nb) + 8, cw * (c % nb) : cw * (c % nb + 1)] = fin[c]
+        rg_ref[chunk(c)] = fin[c]
 
     for phase, ref in enumerate((sx, sg)):
         for h in range(2):
@@ -405,7 +443,8 @@
 
     for copy in links.values():
         copy.wait_send()
-    wait_bytes(r1, s_ar.at[0])
+    wait_bytes(r1.at[pl.ds(0, dpn - 1)], s_ar.at[0])
+    wait_bytes(so.at[pl.ds(0, groups - 1)], s_ar.at[4])
     wait_bytes(ax.at[pl.ds(0, nx - 1)], s_ar.at[1])
     wait_bytes(ay.at[pl.ds(0, yn - 1)], s_ar.at[2])
     wait_bytes(fin.at[pl.ds(0, dpn - 1)], s_ar.at[3])
@@ -437,16 +476,19 @@
             pltpu.VMEM((groups * ROWS, d), BF16),
             pltpu.VMEM((groups * ROWS, ff), F32),
             pltpu.VMEM((groups * ROWS, ff), F32),
+            pltpu.VMEM((groups * ROWS, ff), F32),
+            pltpu.VMEM((groups, 1, LANES), F32),
+            pltpu.VMEM((groups, 1, LANES), F32),
             pltpu.VMEM((3, shard, ff), BF16),
             pltpu.VMEM((3, dpn, shard, ff), BF16),
             pltpu.VMEM((32, d), F32),
-            pltpu.VMEM((dpn - 1, 8, wide), F32),
+            pltpu.VMEM((dpn, 8, wide), F32),
             pltpu.VMEM((cpn // 2, 8, wide), F32),
             pltpu.VMEM((2 * tpn, 8, wide), F32),
             pltpu.VMEM((dpn, 8, wide), F32),
             dma((4,)), dma((4,)), dma((4,)), dma((2,)),
             dma((3 * nz,)), dma((3 * nz,)), dma((3,)), dma((3,)), dma((3,)),
-            dma((4,)), dma((4,)),
+            dma((5,)), dma((5,)),
         ],
         compiler_params=pltpu.CompilerParams(collective_id=0, has_side_effects=True),
         name="experts",

time: 91.8 us -> 81.7 us (0.89)
  Pallas kernels: 87.6 us -> 77.5 us
    pallas_call x1, Pallas kernels: 87.6 us -> 77.5 us  [on_device(): pl.pallas_call(functools.partial(kernel, sizes), out_shape=(jax.ShapeDtyp...]
where the time goes in v4:
time: 81.7 us; the launch traced here: 81.5 us
  Pallas kernels  77.5 us (95%)
  local copies, waits for them, and re-layouts  3.37 us (4%)
    pallas_call x1, Pallas kernels, on_device(): pl.pallas_call(functools.partial(kernel, sizes), out_shape=(jax.ShapeDtyp...  77.5 us
    unnamed x7, local copies, waits for them, and re-layouts  3.37 us

profile of v4, /device:TPU:1, one launch (start us, length us, event | category | flops | bytes accessed | tf_op | source)
XLA Modules:
  0.0 81.5 jit_solution(10401267542594867000)
XLA Ops:
  0.6 77.5 %experts.1 = (bf16[128,1024]{1,0:T(8,128)(2,1)}, bf16[128,1024]{1,0:T(8,128)(2,1)}, f32[32,1024]{1,0:T(8,128)}) custom-call(bf16[128,1024]{1,0:T(8,128)(2,1)} %tok_ref.1, s32[2,128]{1,0:T(2,128)} %bitcast.7, bf16[32,1024]{1,0:T(8,128)(2,1)} %bitcast.5, bf16[1,64,384]{2,1,0:T(8,128)(2,1)} %wg_ref.1, bf16[1,64,384]{2,1,0:T(8,128)(2,1)} %wu_ref.1, ...), custom_call_target="tpu_custom_call" | custom-call | tf_op jit(solution)/shard_map/experts/pallas_call | solution.py:464
  78.1 0.0 copy-start
  78.1 1.7 %copy.13 = bf16[128,1024]{1,0:T(8,128)(2,1)} copy(bf16[128,1024]{1,0:T(8,128)(2,1)} %get-tuple-element.12) | data formatting | bytes 524288
  79.8 0.0 copy-done
  79.8 0.0 copy-start.1
  79.8 0.7 copy.14
  80.5 0.3 copy-done.1
  80.8 0.7 copy.15
Async XLA Ops:
  78.1 1.7 %copy-start = (bf16[128,1024]{1,0:T(8,128)(2,1)S(1)}, bf16[128,1024]{1,0:T(8,128)(2,1)}, u32[]{:S(2)}) copy-start(bf16[128,1024]{1,0:T(8,128)(2,1)} %get-tuple-element.13) | copy-start | bytes 786436
  79.8 1.0 %copy-start.1 = (f32[32,1024]{1,0:T(8,128)S(1)}, f32[32,1024]{1,0:T(8,128)}, u32[]{:S(2)}) copy-start(f32[32,1024]{1,0:T(8,128)} %get-tuple-element.8) | copy-start | bytes 393220

commit v5 on v4

--- a/solution.py
+++ b/solution.py
@@ -31,8 +31,8 @@
     sizes,
     tok_ref, ids_ref, rw_ref, wg_ref, wu_ref, wd_ref, g_ref,
     moe_ref, gt_ref, rg_ref,
-    sx, sg, rx, rg, px, pg, cx, cg, xs, gs, act, up, gh, so, si, ws, w, part, r1, ax, ay, fin,
-    s_in, r_in, s_out, r_out, s_ring, r_ring, s_far, s_pair, r_own, s_ar, r_ar,
+    sx, sg, rx, rg, px, pg, cx, cg, xs, gs, act, up, gh, so, si, ws, wr, w, part, r1, ax, ay, fin,
+    s_in, r_in, s_out, r_out, s_ring, r_ring, s_far, s_mid, s_pair, r_mid, r_own, s_ar, r_ar,
 ):
     dpn, tpn, cpn = sizes
     groups = tpn * cpn
@@ -165,10 +165,19 @@
 
     pl.semaphore_wait(barrier, 2 * groups - 1 + dpn - 2)
 
+    hop = (yn // 4) * (1 - 2 * core)
+    hop_tp, hop_base = column(lax.rem(y + hop + yn, yn))
+    from_yh = lax.rem(y - hop + yn, yn) // tpn
+
     def far(i):
         return remote(
-            ws.at[i], w.at[i, dp], s_far.at[i], r_own.at[i],
-            (z * 2 + yh, tp, (1 - yh) * nx + xi),
+            ws.at[i], wr.at[i], s_far.at[i], r_mid.at[i], (dp, hop_tp, hop_base + xi)
+        )
+
+    def relay(i):
+        return remote(
+            wr.at[i], w.at[i, dp], s_mid.at[i], r_own.at[i],
+            (z * 2 + from_yh, hop_tp, hop_base + xi),
         )
 
     def pair(i):
@@ -222,24 +231,27 @@
                 src.at[expert], dst.at[r], s_in.at[index], r_in.at[index], to
             ).start())
 
-    send_in(sx, rx, 0)
-
     @pl.when(core == yh)
     def _():
         for i in range(3):
             wait_bytes(w.at[i, pl.ds(0, 1)], r_own.at[i])
         enter_ring()
 
+    for i in range(3):
+        far(i).wait_recv()
+        relay(i).start()
     pack_home(grads, sg)
-    send_in(sg, rg, 1)
-    rx[0] = sx[mine]
-    rg[0] = sg[mine]
 
     @pl.when(core != yh)
     def _():
         for i in range(3):
             wait_bytes(w.at[i, pl.ds(0, 2)], r_own.at[i])
         enter_ring()
+
+    send_in(sx, rx, 0)
+    send_in(sg, rg, 1)
+    rx[0] = sx[mine]
+    rg[0] = sg[mine]
 
     logits = mm_t(tokens, rw_ref[...])
     ecount = rw_ref.shape[0]
@@ -435,6 +447,7 @@
             wait_bytes(ref.at[pl.ds(lo, half * (h + 1) - lo)], s_out.at[2 * phase + h])
     for i in range(3):
         far(i).wait_send()
+        relay(i).wait_send()
 
     @pl.when(core != yh)
     def _():
@@ -480,6 +493,7 @@
             pltpu.VMEM((groups, 1, LANES), F32),
             pltpu.VMEM((groups, 1, LANES), F32),
             pltpu.VMEM((3, shard, ff), BF16),
+            pltpu.VMEM((3, shard, ff), BF16),
             pltpu.VMEM((3, dpn, shard, ff), BF16),
             pltpu.VMEM((32, d), F32),
             pltpu.VMEM((dpn, 8, wide), F32),
@@ -487,7 +501,8 @@
             pltpu.VMEM((2 * tpn, 8, wide), F32),
             pltpu.VMEM((dpn, 8, wide), F32),
             dma((4,)), dma((4,)), dma((4,)), dma((2,)),
-            dma((3 * nz,)), dma((3 * nz,)), dma((3,)), dma((3,)), dma((3,)),
+            dma((3 * nz,)), dma((3 * nz,)),
+            dma((3,)), dma((3,)), dma((3,)), dma((3,)), dma((3,)),
             dma((5,)), dma((5,)),
         ],
         compiler_params=pltpu.CompilerParams(collective_id=0, has_side_effects=True),

time: 81.7 us -> 85 us (1.040)
  Pallas kernels: 77.5 us -> 80.8 us
    pallas_call x1, Pallas kernels: 77.5 us -> 80.8 us  [on_device(): pl.pallas_call(functools.partial(kernel, sizes), out_shape=(jax.ShapeDtyp...]
where the time goes in v5:
time: 85 us; the launch traced here: 84.8 us
  Pallas kernels  80.8 us (95%)
  local copies, waits for them, and re-layouts  3.37 us (4%)
    pallas_call x1, Pallas kernels, on_device(): pl.pallas_call(functools.partial(kernel, sizes), out_shape=(jax.ShapeDtyp...  80.8 us
    unnamed x7, local copies, waits for them, and re-layouts  3.37 us

profile of v5, /device:TPU:1, one launch (start us, length us, event | category | flops | bytes accessed | tf_op | source)
XLA Modules:
  0.0 84.8 jit_solution(3781829982312456629)
XLA Ops:
  0.6 80.8 %experts.1 = (bf16[128,1024]{1,0:T(8,128)(2,1)}, bf16[128,1024]{1,0:T(8,128)(2,1)}, f32[32,1024]{1,0:T(8,128)}) custom-call(bf16[128,1024]{1,0:T(8,128)(2,1)} %tok_ref.1, s32[2,128]{1,0:T(2,128)} %bitcast.7, bf16[32,1024]{1,0:T(8,128)(2,1)} %bitcast.5, bf16[1,64,384]{2,1,0:T(8,128)(2,1)} %wg_ref.1, bf16[1,64,384]{2,1,0:T(8,128)(2,1)} %wu_ref.1, ...), custom_call_target="tpu_custom_call" | custom-call | tf_op jit(solution)/shard_map/experts/pallas_call | solution.py:477
  81.4 0.0 copy-start
  81.4 1.7 %copy.13 = bf16[128,1024]{1,0:T(8,128)(2,1)} copy(bf16[128,1024]{1,0:T(8,128)(2,1)} %get-tuple-element.12) | data formatting | bytes 524288
  83.1 0.0 copy-done
  83.1 0.0 copy-start.1
  83.1 0.7 copy.14
  83.8 0.3 copy-done.1
  84.1 0.7 copy.15
Async XLA Ops:
  81.4 1.7 %copy-start = (bf16[128,1024]{1,0:T(8,128)(2,1)S(1)}, bf16[128,1024]{1,0:T(8,128)(2,1)}, u32[]{:S(2)}) copy-start(bf16[128,1024]{1,0:T(8,128)(2,1)} %get-tuple-element.13) | copy-start | bytes 786436
  83.1 1.0 %copy-start.1 = (f32[32,1024]{1,0:T(8,128)S(1)}, f32[32,1024]{1,0:T(8,128)}, u32[]{:S(2)}) copy-start(f32[32,1024]{1,0:T(8,128)} %get-tuple-element.8) | copy-start | bytes 393220

commit v6 on v5

--- a/solution.py
+++ b/solution.py
@@ -240,7 +240,7 @@
     for i in range(3):
         far(i).wait_recv()
         relay(i).start()
-    pack_home(grads, sg)
+    send_in(sx, rx, 0)
 
     @pl.when(core != yh)
     def _():
@@ -248,7 +248,7 @@
             wait_bytes(w.at[i, pl.ds(0, 2)], r_own.at[i])
         enter_ring()
 
-    send_in(sx, rx, 0)
+    pack_home(grads, sg)
     send_in(sg, rg, 1)
     rx[0] = sx[mine]
     rg[0] = sg[mine]

time: 85 us -> 83.5 us (0.982)
  Pallas kernels: 80.8 us -> 79.3 us
    pallas_call x1, Pallas kernels: 80.8 us -> 79.3 us  [on_device(): pl.pallas_call(functools.partial(kernel, sizes), out_shape=(jax.ShapeDtyp...]
where the time goes in v6:
time: 83.5 us; the launch traced here: 83.3 us
  Pallas kernels  79.3 us (95%)
  local copies, waits for them, and re-layouts  3.37 us (4%)
    pallas_call x1, Pallas kernels, on_device(): pl.pallas_call(functools.partial(kernel, sizes), out_shape=(jax.ShapeDtyp...  79.3 us
    unnamed x7, local copies, waits for them, and re-layouts  3.37 us

profile of v6, /device:TPU:1, one launch (start us, length us, event | category | flops | bytes accessed | tf_op | source)
XLA Modules:
  0.0 83.3 jit_solution(17958732894790831634)
XLA Ops:
  0.6 79.3 %experts.1 = (bf16[128,1024]{1,0:T(8,128)(2,1)}, bf16[128,1024]{1,0:T(8,128)(2,1)}, f32[32,1024]{1,0:T(8,128)}) custom-call(bf16[128,1024]{1,0:T(8,128)(2,1)} %tok_ref.1, s32[2,128]{1,0:T(2,128)} %bitcast.7, bf16[32,1024]{1,0:T(8,128)(2,1)} %bitcast.5, bf16[1,64,384]{2,1,0:T(8,128)(2,1)} %wg_ref.1, bf16[1,64,384]{2,1,0:T(8,128)(2,1)} %wu_ref.1, ...), custom_call_target="tpu_custom_call" | custom-call | tf_op jit(solution)/shard_map/experts/pallas_call | solution.py:477
  80.0 0.0 copy-start
  80.0 1.7 %copy.13 = bf16[128,1024]{1,0:T(8,128)(2,1)} copy(bf16[128,1024]{1,0:T(8,128)(2,1)} %get-tuple-element.12) | data formatting | bytes 524288
  81.7 0.0 copy-done
  81.7 0.0 copy-start.1
  81.7 0.7 copy.14
  82.4 0.3 copy-done.1
  82.7 0.7 copy.15
Async XLA Ops:
  80.0 1.7 %copy-start = (bf16[128,1024]{1,0:T(8,128)(2,1)S(1)}, bf16[128,1024]{1,0:T(8,128)(2,1)}, u32[]{:S(2)}) copy-start(bf16[128,1024]{1,0:T(8,128)(2,1)} %get-tuple-element.13) | copy-start | bytes 786436
  81.7 1.0 %copy-start.1 = (f32[32,1024]{1,0:T(8,128)S(1)}, f32[32,1024]{1,0:T(8,128)}, u32[]{:S(2)}) copy-start(f32[32,1024]{1,0:T(8,128)} %get-tuple-element.8) | copy-start | bytes 393220
